TPU v7x, 512 devices: a whole 4x8x8 slice. The times are simulated.
512 devices in a mesh: leaf: 64 (over y, x, core), probe: 8 (over z).
Axes of the slice: x: 4, y: 8, z: 8, core: 2. Of those that a mesh axis runs over, the one named last changes fastest.
Arguments:
- coef_fine: bfloat16 [64, 262144], P('probe', 'leaf'), may hold values from -0.59765625 to 0.59765625
- points_fine: float32 [3, 262144], P(None, 'leaf'), may hold values from -1 to 1
- points_coarse: float32 [3, 131072], P(None, 'leaf'), may hold values from -1 to 1
- transfer: bfloat16 [64, 262144], P(None, 'leaf'), may hold values from -0.5 to 0.5
- send_fine: int32 [64, 64, 16], P('leaf'), may hold values from 0 to 63, as said below
- slots_fine: int32 [4096, 64], P('leaf'), may hold values from 0 to 1087, as said below
- counts_fine: int32 [4096], P('leaf'), may hold values from 1 to 64, as said below
- send_coarse: int32 [64, 64, 8], P('leaf'), may hold values from 0 to 31, as said below
- slots_coarse: int32 [2048, 64], P('leaf'), may hold values from 0 to 543, as said below
- counts_coarse: int32 [2048], P('leaf'), may hold values from 1 to 64, as said below
Outputs:
- far_field: float32 [64, 262144], P('probe', 'leaf')
- probe_gram: float32 [64, 64], P('probe')
Inputs may be any that keep to these rules, and one draw needn't show every extreme that they name: `send_fine`: entry [e, d, i] is the local index of a cluster of device e that device e sends to device d; every device sends exactly 16 distinct clusters to every device, itself included. `slots_fine`: A slot value v below 64 names the owning device's own cluster v; a value of 64 or more names entry [(v - 64) // 16, owner, (v - 64) % 16] of send_fine. Only the first counts_fine[c] slots of cluster c are live; every device has a cluster with all 64 slots live. `send_coarse`: entry [e, d, i] is the local index of a cluster of device e that device e sends to device d; every device sends exactly 8 distinct clusters to every device, itself included. `slots_coarse`: A slot value v below 32 names the owning device's own cluster v; a value of 32 or more names entry [(v - 32) // 8, owner, (v - 32) % 8] of send_coarse. Only the first counts_coarse[q] slots of cluster q are live; every device has a cluster with all 64 slots live.
All inputs are finite; a program needn't handle non-finite values.
Results may differ from a plain program's by a relative error of at most 0.0036.
Values may be sent and summed in bfloat16 or wider, within the bound.
A program may use at most 64 MiB of HBM per device.

v0:
```python
import math

import jax
import jax.numpy as jnp
from jax import lax
from jax.sharding import PartitionSpec as P

kernel_rate = 1.5


def gaussian_tiles(target_points, source_points):
    squared = jnp.zeros(
        (
            source_points.shape[0],
            source_points.shape[1],
            target_points.shape[2],
            source_points.shape[3],
        ),
        jnp.float32,
    )
    for coord in range(3):
        coord_delta = target_points[:, None, coord, :, None] - source_points[:, :, coord, None, :]
        squared = squared + coord_delta * coord_delta
    return jnp.exp(-kernel_rate * squared)


def level_sweep(table_coef, table_points, own_points, slot_table, count_table):
    clusters, pair_slots = slot_table.shape
    group_size = math.gcd(clusters, max(1, 256 // pair_slots))
    turns = clusters // group_size
    rank_width = own_points.shape[2]

    def one_group(group_item):
        slot_group, count_group, target_points = group_item
        partner_coef = table_coef[slot_group]
        partner_points = table_points[slot_group]
        kernel_values = gaussian_tiles(target_points, partner_points)
        live_mask = lax.broadcasted_iota(jnp.int32, slot_group.shape, 1) < count_group[:, None]
        weights = jnp.where(live_mask[:, :, None, None], kernel_values, 0.0).astype(jnp.bfloat16)
        return jnp.einsum(
            "gmkj,gmpj->gpk", weights, partner_coef, preferred_element_type=jnp.float32
        )

    result = lax.map(
        one_group,
        (
            slot_table.reshape(turns, group_size, pair_slots),
            count_table.reshape(turns, group_size),
            own_points.reshape(turns, group_size, 3, rank_width),
        ),
    )
    return result.reshape(clusters, table_coef.shape[1], table_coef.shape[2])


def shards(
    coef_fine,
    points_fine,
    points_coarse,
    transfer,
    send_fine,
    slots_fine,
    counts_fine,
    send_coarse,
    slots_coarse,
    counts_coarse,
):
    rank_width = transfer.shape[0]
    probes = coef_fine.shape[0]
    fine_count = counts_fine.shape[0]
    coarse_count = counts_coarse.shape[0]
    owners = lax.axis_size("leaf")
    fine_rows = coef_fine.reshape(probes, fine_count, rank_width).transpose(1, 0, 2)
    fine_points = points_fine.reshape(3, fine_count, rank_width).transpose(1, 0, 2)
    coarse_points = points_coarse.reshape(3, coarse_count, rank_width).transpose(1, 0, 2)
    fine_lists = send_fine.reshape(owners, -1)
    coarse_lists = send_coarse.reshape(owners, -1)
    fine_point_pack = fine_points[fine_lists].reshape(owners, -1)
    fine_coef_pack = fine_rows[fine_lists].reshape(owners, -1)
    coarse_point_pack = coarse_points[coarse_lists].reshape(owners, -1)
    fine_point_in, coarse_point_in = (
        lax.all_to_all(fine_point_pack, "leaf", split_axis=0, concat_axis=0, tiled=True),
        lax.all_to_all(coarse_point_pack, "leaf", split_axis=0, concat_axis=0, tiled=True),
    )
    fine_coef_in = lax.all_to_all(fine_coef_pack, "leaf", split_axis=0, concat_axis=0, tiled=True)
    matrices = transfer.reshape(rank_width, coarse_count, 2, rank_width)
    children = coef_fine.reshape(probes, coarse_count, 2, rank_width)
    coarse_rows = jnp.einsum(
        "pqck,kqcj->qpj", children, matrices, preferred_element_type=jnp.float32
    ).astype(jnp.bfloat16)
    coarse_coef_pack = coarse_rows[coarse_lists].reshape(owners, -1)
    coarse_coef_in = lax.all_to_all(
        coarse_coef_pack, "leaf", split_axis=0, concat_axis=0, tiled=True
    )
    coarse_table = jnp.concatenate(
        [coarse_rows, coarse_coef_in.reshape(-1, probes, rank_width)], axis=0
    )
    coarse_point_table = jnp.concatenate(
        [coarse_points, coarse_point_in.reshape(-1, 3, rank_width)], axis=0
    )
    fine_table = jnp.concatenate([fine_rows, fine_coef_in.reshape(-1, probes, rank_width)], axis=0)
    fine_point_table = jnp.concatenate(
        [fine_points, fine_point_in.reshape(-1, 3, rank_width)], axis=0
    )
    coarse_far = level_sweep(
        coarse_table, coarse_point_table, coarse_points, slots_coarse, counts_coarse
    )
    fine_far = level_sweep(fine_table, fine_point_table, fine_points, slots_fine, counts_fine)
    downward = jnp.einsum(
        "qpj,kqcj->qcpk",
        coarse_far.astype(jnp.bfloat16),
        matrices,
        preferred_element_type=jnp.float32,
    ).reshape(fine_count, probes, rank_width)
    combined = fine_far + downward
    far_field = combined.transpose(1, 0, 2).reshape(probes, fine_count * rank_width)
    coef_single = coef_fine.astype(jnp.float32)
    partial_gram = lax.dot_general(
        coef_single,
        lax.all_gather(far_field, "probe", axis=0, tiled=True),
        (((1,), (1,)), ((), ())),
        precision=lax.Precision.HIGHEST,
    )
    gram_scale = 1.0 / math.sqrt(owners * fine_count * rank_width)
    probe_gram = lax.psum(partial_gram, "leaf") * gram_scale
    return (far_field, probe_gram)


def solution(mesh):
    return jax.shard_map(
        shards,
        mesh=mesh,
        in_specs=(
            P("probe", "leaf"),
            P(None, "leaf"),
            P(None, "leaf"),
            P(None, "leaf"),
            P("leaf", None, None),
            P("leaf", None),
            P("leaf"),
            P("leaf", None, None),
            P("leaf", None),
            P("leaf"),
        ),
        out_specs=(P("probe", "leaf"), P("probe", None)),
        check_vma=False,
    )
```

profile of v0, /device:TPU:1, one launch (start us, length us, event | category | flops | bytes accessed | tf_op | source)
XLA Modules:
  0.0 563.6 jit_solution(7789410246560961150)
XLA Ops:
  12.6 11.8 %all-to-all-start.3 = ((f32[64,1,1536]{2,1,0:T(1,128)}), f32[64,1,1536]{2,1,0:T(1,128)}, u32[]{:S(2)}, u32[]{:S(2)}) async-start(f32[64,1,1536]{2,1,0:T(1,128)} %all_to_all.35), calls=%async_computation.3 | async-start | bytes 786432 | tf_op jit(solution)/shard_map/all_to_all | solution.py:82
  29.6 3.7 reduce.4
  34.4 5.0 all-to-all-done.3
  39.5 5.4 all-to-all-start.2
  45.3 3.6 gather_fusion.5
  51.2 11.4 %all-to-all-done.2 = bf16[64,2,2048]{2,1,0:T(2,128)(2,1)S(1)} async-done(((bf16[64,2,2048]{2,1,0:T(2,128)(2,1)}), bf16[64,2,2048]{2,1,0:T(2,128)(2,1)S(1)}, u32[]{:S(2)}, u32[]{:S(2)}) %all-to-all-start.2) | async-done | bytes 524320 | tf_op jit(solution)/shard_map/all_to_all | solution.py:91
  62.6 5.9 %all-to-all-start.1 = ((f32[64,1,3072]{2,1,0:T(1,128)}), f32[64,1,3072]{2,1,0:T(1,128)}, u32[]{:S(2)}, u32[]{:S(2)}) async-start(f32[64,1,3072]{2,1,0:T(1,128)} %all_to_all.33), calls=%async_computation.1 | async-start | bytes 1572864 | tf_op jit(solution)/shard_map/all_to_all | solution.py:81
  71.0 7.5 %gather_fusion.4 = bf16[1024,8,64]{2,1,0:T(8,128)(2,1)} fusion(bf16[64,8,64]{2,1,0:T(8,128)(2,1)S(1)} %bitcast.144, s32[1024]{0:T(1024)S(1)} %broadcast_clamp_fusion), kind=kCustom, calls=%fused_computation.4 | custom fusion | bytes 2101248 | tf_op jit(solution)/shard_map/gather | solution.py:78
  78.5 6.6 %all_to_all.32 = bf16[64,1,8192]{2,1,0:T(2,128)(2,1)S(1)} reshape(bf16[1024,8,64]{2,1,0:T(8,128)(2,1)} %gather_fusion.4) | data formatting | bytes 2097152 | tf_op jit(solution)/shard_map/all_to_all | solution.py:84
  85.1 8.1 %reduce.5 = bf16[64,8192]{1,0:T(8,128)(2,1)} reduce(bf16[64,1,8192]{2,1,0:T(2,128)(2,1)S(1)} %all_to_all.32, bf16[]{:T(256)} %broadcast.160), dimensions={1}, to_apply=%all_to_all.32.reduce_sub_computation | reduce | bytes 2097154 | tf_op jit(solution)/shard_map/all_to_all | solution.py:84
  93.3 2.6 reshape.356
  100.9 4.0 reduce.2
  107.2 10.5 %all-to-all-start = ((bf16[64,2,4096]{2,1,0:T(2,128)(2,1)}), bf16[64,2,4096]{2,1,0:T(2,128)(2,1)}, u32[]{:S(2)}, u32[]{:S(2)}) async-start(bf16[64,2,4096]{2,1,0:T(2,128)(2,1)} %reshape.356), calls=%async_computation | async-start | bytes 2097152 | tf_op jit(solution)/shard_map/all_to_all | solution.py:84
  117.7 68.1 %while.21 = (s32[]{:T(128)}, bf16[8,4,8,64]{3,2,1,0:T(8,128)(2,1)}, s32[8,4,64]{2,1,0:T(4,128)}, bf16[544,8,64]{2,1,0:T(8,128)(2,1)S(1)}, s32[8,4]{1,0:T(8,128)S...) while((s32[]{:T(128)}, bf16[8,4,8,64]{3,2,1,0:T(8,128)(2,1)}, ...), condition=%wide.region_3.4_spmd, body=%wide.region_2.3_spmd.sunk | while | flops 28313600 | bytes 1813149 | solution.py:44
  121.4 4.8 fusion.41
  130.0 4.8 fusion.41
  138.5 4.8 fusion.41
  147.0 4.8 fusion.41
  155.5 4.8 fusion.41
  164.0 4.8 fusion.41
  172.5 4.8 fusion.41
  181.1 4.8 fusion.41
  185.9 2.9 fusion.15
  188.8 3.0 reduce.1
  197.4 7.7 %reshape.357 = bf16[64,1,8192]{2,1,0:T(2,128)(2,1)} reshape(bf16[64,2,4096]{2,1,0:T(2,128)(2,1)} %all-to-all-done) | data formatting | bytes 2097152
  205.1 7.9 %reduce = bf16[64,8192]{1,0:T(8,128)(2,1)S(1)} reduce(bf16[64,1,8192]{2,1,0:T(2,128)(2,1)} %reshape.357, bf16[]{:T(256)} %constant.57), dimensions={1}, to_apply=%all_to_all.25.reduce_sub_computation | reduce | bytes 2097154 | tf_op jit(solution)/shard_map/all_to_all | solution.py:84
  213.0 3.3 reshape.253
  216.3 3.0 pad_maximum_fusion
  219.3 162.5 %while.20 = (s32[]{:T(128)}, f32[16,4,8,64]{3,2,1,0:T(8,128)}, s32[16,4,64]{2,1,0:T(4,128)}, bf16[1088,8,64]{2,1,0:T(8,128)(2,1)}, s32[16,4]{1,0:T(8,128)S(1)}, ...) while((s32[]{:T(128)}, f32[16,4,8,64]{3,2,1,0:T(8,128)}, s32[16,4,64]{2,1,0:T(4,128)}, ...), condition=%wide.region_1.2_spmd, body=%wide.region_0.1_spmd.sunk | while | flops 28313600 | bytes 1813149 | solution.py:44
  224.7 4.8 fusion.37
  234.8 4.8 fusion.37
  245.0 4.8 fusion.37
  255.1 4.8 fusion.37
  265.3 4.8 fusion.37
  270.9 2.5 gather_fusion
  275.5 4.8 fusion.37
  285.6 4.8 fusion.37
  295.8 4.8 fusion.37
  305.9 4.8 fusion.37
  316.1 4.8 fusion.37
  326.2 4.8 fusion.37
  336.4 4.8 fusion.37
  346.6 4.8 fusion.37
  356.7 4.8 fusion.37
  366.9 4.8 fusion.37
  377.0 4.8 fusion.37
  383.8 41.6 %all-gather.2.cloned.1.call-done = f32[64,4096]{1,0:T(8,128)} async-done(((f32[8,4096]{1,0:T(8,128)}), f32[64,4096]{1,0:T(8,128)}) %all-gather.2.cloned.1.call-update) | async-done | bytes 1048592 | tf_op jit(solution)/shard_map/all_gather | solution.py:119
  427.1 128.7 %psum.7 = f32[8,64]{1,0:T(8,128)S(1)} all-reduce(f32[8,64]{1,0:T(8,128)S(1)} %convolution_bitcast_fusion.1), channel_id=1, replica_groups=mesh['leaf'=64,'probe'=8] {'leaf'}, use_global_device_ids=true, to_apply=%region_4.5 | all-reduce | flops 512 | bytes 4096 | tf_op jit(solution)/shard_map/psum | solution.py:124
  (314 shorter events, 145.9 us)
Async XLA Ops:
  8.9 15.5 %copy-start.4 = (bf16[64,4096]{1,0:T(8,128)(2,1)S(1)}, bf16[64,4096]{1,0:T(8,128)(2,1)}, u32[]{:S(2)}) copy-start(bf16[64,4096]{1,0:T(8,128)(2,1)} %param.17) | copy-start | bytes 1572868
  11.0 14.5 %copy-start.3 = (bf16[8,4096]{1,0:T(8,128)(2,1)S(1)}, bf16[8,4096]{1,0:T(8,128)(2,1)}, u32[]{:S(2)}) copy-start(bf16[8,4096]{1,0:T(8,128)(2,1)} %param.14) | copy-start | bytes 196612
  12.6 26.9 %all-to-all-start.3 = ((f32[64,1,1536]{2,1,0:T(1,128)}), f32[64,1,1536]{2,1,0:T(1,128)}, u32[]{:S(2)}, u32[]{:S(2)}) async-start(f32[64,1,1536]{2,1,0:T(1,128)} %all_to_all.35), calls=%async_computation.3 | async-start | bytes 786432 | tf_op jit(solution)/shard_map/all_to_all | solution.py:82
  25.5 3.5 copy-start
  29.0 15.9 %copy-start.8 = (s32[1,64,16]{1,2,0:T(8,128)S(1)}, s32[1,64,16]{1,2,0:T(8,128)}, u32[]{:S(2)}) copy-start(s32[1,64,16]{1,2,0:T(8,128)} %param.18) | copy-start | bytes 12292
  29.0 16.1 %copy-start.7 = (f32[3,4096]{1,0:T(4,128)S(1)}, f32[3,4096]{1,0:T(4,128)}, u32[]{:S(2)}) copy-start(f32[3,4096]{1,0:T(4,128)} %param.15) | copy-start | bytes 147460
  39.5 23.1 %all-to-all-start.2 = ((bf16[64,2,2048]{2,1,0:T(2,128)(2,1)}), bf16[64,2,2048]{2,1,0:T(2,128)(2,1)S(1)}, u32[]{:S(2)}, u32[]{:S(2)}) async-start(bf16[64,2,2048]{2,1,0:T(2,128)(2,1)} %reshape.354), calls=%async_computation.2 | async-start | bytes 1048576 | tf_op jit(solution)/shard_map/all_to_all | solution.py:91
  48.9 21.3 %copy-start.9 = (s32[32]{0:T(128)S(1)}, s32[32]{0:T(128)}, u32[]{:S(2)}) copy-start(s32[32]{0:T(128)} %param.23) | copy-start | bytes 388
  62.6 15.9 %copy-start.1 = (bf16[64,2,2048]{2,1,0:T(2,128)(2,1)}, bf16[64,2,2048]{2,1,0:T(2,128)(2,1)S(1)}, u32[]{:S(2)}) copy-start(bf16[64,2,2048]{2,1,0:T(2,128)(2,1)S(1)} %all-to-all-done.2) | copy-start | bytes 1572868
  62.6 44.6 %all-to-all-start.1 = ((f32[64,1,3072]{2,1,0:T(1,128)}), f32[64,1,3072]{2,1,0:T(1,128)}, u32[]{:S(2)}, u32[]{:S(2)}) async-start(f32[64,1,3072]{2,1,0:T(1,128)} %all_to_all.33), calls=%async_computation.1 | async-start | bytes 1572864 | tf_op jit(solution)/shard_map/all_to_all | solution.py:81
  85.1 10.7 %copy-start.10 = (s32[64]{0:T(128)S(1)}, s32[64]{0:T(128)}, u32[]{:S(2)}) copy-start(s32[64]{0:T(128)} %param.20) | copy-start | bytes 772
  95.9 3.6 copy-start.6
  99.2 1.0 copy-start.2
  107.2 90.2 %all-to-all-start = ((bf16[64,2,4096]{2,1,0:T(2,128)(2,1)}), bf16[64,2,4096]{2,1,0:T(2,128)(2,1)}, u32[]{:S(2)}, u32[]{:S(2)}) async-start(bf16[64,2,4096]{2,1,0:T(2,128)(2,1)} %reshape.356), calls=%async_computation | async-start | bytes 2097152 | tf_op jit(solution)/shard_map/all_to_all | solution.py:84
  117.7 307.7 %all-gather.2.cloned.1.call-start = ((), (), s32[]{:S(2)}) async-start(), calls=%async_computation.4 | async-start | bytes 1179648 | tf_op jit(solution)/shard_map/all_gather | solution.py:119
  191.8 2.7 copy-start.5
Sparse Core Ops, SparseCore 0:
  383.9 41.4 all-gather.1
where the time goes:
time: 575 us; the launch traced here: 564 us
  local copies, waits for them, and re-layouts  152 us (26%)
  blocking collectives  129 us (22%)
  matrix products  121 us (21%)
  waiting for transfers between devices  58 us (10%)
  other arithmetic  54.3 us (9%)
  starting transfers between devices  33.6 us (6%)
  between operations  14.6 us (3%)
    psum x1, blocking collectives, shards(): probe_gram = lax.psum(partial_gram, 'leaf') * gram_scale  129 us
    dot_general x24, matrix products, one_group(): jnp.einsum('gmkj,gmpj->gpk', weights, partner_coef, preferred_element_typ...  116 us
    gather x24, local copies, waits for them, and re-layouts, one_group(): partner_coef = table_coef[slot_group]  45.7 us
    all_gather x1, waiting for transfers between devices, shards(): lax.all_gather(far_field, 'probe', axis=0, tiled=True)  41.6 us
    gather x24, local copies, waits for them, and re-layouts, one_group(): partner_points = table_points[slot_group]  23.9 us
    squeeze x24, local copies, waits for them, and re-layouts, level_sweep(): lax.map(one_group, (slot_table.reshape(turns, group_size, pair_slots), co...  16.8 us
    select_n x24, other arithmetic, one_group(): partner_coef = table_coef[slot_group]  16.4 us
    all_to_all x2, other arithmetic, shards(): lax.all_to_all(fine_coef_pack, 'leaf', split_axis=0, concat_axis=0, tiled...  16 us
  transfers between devices with their start and end apart: 5, of which 3 were waited for; matrix products, arithmetic and copies ran while one was open for 22% of the time, Pallas kernels for 0%

commit v1 on v0

v1 whole, which is shorter than its diff:
```python
import functools
import math

import jax
import jax.numpy as jnp
from jax import lax
from jax.experimental import pallas as pl
from jax.experimental.pallas import tpu as pltpu
from jax.sharding import PartitionSpec as P

kernel_rate = 1.5
LOG2E = 1.4426950408889634
RANK = 64
NX, NY, NZ = 4, 8, 8
CHIPS = NX * NY
FINE, COARSE, PAIRS = 64, 32, 64
FT, CT = FINE // 2, COARSE // 2
TILES = FT + CT + 1
LIST_TILE = FT + CT
ROWS = 2 * CHIPS * TILES
ZERO = ROWS
SPAN = ROWS + 8
MESH = pl.DeviceIdType.MESH
F32, BF16 = jnp.float32, jnp.bfloat16
NT = (((1,), (1,)), ((), ()))
VMEM_LIMIT = 60 * 1024 * 1024


def features(points):
    high = points.astype(BF16).astype(F32)
    low = (points - high).astype(BF16).astype(F32)
    squares = points[0:1] * points[0:1] + points[1:2] * points[1:2] + points[2:3] * points[2:3]
    bias = squares * (-kernel_rate * LOG2E)
    bias_high = bias.astype(BF16).astype(F32)
    bias_low = (bias - bias_high).astype(BF16).astype(F32)
    scaled = points * (2.0 * kernel_rate * LOG2E)
    scaled_high = scaled.astype(BF16).astype(F32)
    scaled_low = (scaled - scaled_high).astype(BF16).astype(F32)
    ones = jnp.ones((2, points.shape[1]), F32)
    nothing = jnp.zeros((8, points.shape[1]), F32)
    source = jnp.concatenate([high, low, bias_high, bias_low], axis=0)
    target = jnp.concatenate(
        [
            scaled_high,
            scaled_high,
            ones,
            nothing,
            scaled_low,
            scaled_low,
            nothing[0:2],
            nothing,
        ],
        axis=0,
    )
    return source, target, jnp.exp(squares * -kernel_rate)


def prep_kernel(coef, fine_pts, coarse_pts, transfer, lists, payload, target_out, scale_out):
    source, target, scale = features(fine_pts[...])
    rows = jnp.concatenate([source, coef[...].astype(F32)], axis=0).astype(BF16)
    target = target.astype(BF16)
    for t in range(FT):
        cut = slice(t * 128, t * 128 + 128)
        payload[t] = rows[:, cut]
        target_out[t] = target[:, cut]
    scale_out[:, 0 : FT * 128] = jnp.broadcast_to(scale, (8, FT * 128))
    source, target, scale = features(coarse_pts[...])
    target = target.astype(BF16)
    for t in range(CT):
        halves = []
        for q in (2 * t, 2 * t + 1):
            mats = transfer[:, q * 128 : q * 128 + 128]
            left = jnp.dot(
                coef[:, q * 128 : q * 128 + 64], mats, preferred_element_type=F32
            )
            right = jnp.dot(
                coef[:, q * 128 + 64 : q * 128 + 128], mats, preferred_element_type=F32
            )
            halves.append(left[:, 0:64] + right[:, 64:128])
        cut = slice(t * 128, t * 128 + 128)
        rows = jnp.concatenate([source[:, cut], jnp.concatenate(halves, axis=1)], axis=0)
        payload[FT + t] = rows.astype(BF16)
        target_out[FT + t] = target[:, cut]
    scale_out[:, FT * 128 :] = jnp.broadcast_to(scale, (8, CT * 128))
    payload[LIST_TILE] = lists[...]


def prep(coef, fine_pts, coarse_pts, transfer, lists):
    return pl.pallas_call(
        prep_kernel,
        out_shape=(
            jax.ShapeDtypeStruct((TILES, 16, 128), BF16),
            jax.ShapeDtypeStruct((FT + CT, 32, 128), BF16),
            jax.ShapeDtypeStruct((8, (FT + CT) * 128), F32),
        ),
        compiler_params=pltpu.CompilerParams(vmem_limit_bytes=VMEM_LIMIT),
        name="prep",
    )(coef, fine_pts, coarse_pts, transfer, lists)


FLOWS = (
    (True, 1, 0, 10),
    (True, -1, 10, 20),
    (False, 1, 20, 35),
    (False, -1, 35, 49),
)


def spread_kernel(
    payload, coef, table, probes, link_recv, link_send, chip_recv, chip_send, z_recv, z_send, own_sem
):
    leaf = lax.axis_index("leaf")
    z = lax.axis_index("probe")
    core = lax.rem(leaf, 2)
    chip = leaf // 2
    x = lax.rem(chip, NX)
    y = chip // NX

    def chip_at(xs, ys):
        return lax.rem(y + ys + NY, NY) * NX + lax.rem(x + xs + NX, NX)

    def leaf_at(xs, ys):
        return chip_at(xs, ys) * 2 + core

    twin = chip * 2 + (1 - core)
    barrier = pltpu.get_barrier_semaphore()
    peers = [leaf_at(1, 0), leaf_at(-1, 0), leaf_at(0, 1), leaf_at(0, -1), twin]
    for peer in peers:
        pl.semaphore_signal(barrier, 1, device_id={"leaf": peer}, device_id_type=MESH)
    for s in range(1, NZ):
        pl.semaphore_signal(
            barrier, 1, device_id={"probe": lax.rem(z + s, NZ)}, device_id_type=MESH
        )
    pl.semaphore_wait(barrier, len(peers) + NZ - 1)

    own = pltpu.make_async_copy(payload, table.at[core, chip], own_sem.at[0])
    own.start()
    own_coef = pltpu.make_async_copy(coef, probes.at[z], own_sem.at[1])
    own_coef.start()

    def piece(f, i, j):
        _, sign, low, high = FLOWS[f]
        return table.at[core, chip_at(-sign * i, -sign * j), low:high]

    def source(f, i, j):
        _, _, low, high = FLOWS[f]
        return payload.at[low:high] if i == 0 and j == 0 else piece(f, i, j)

    def push(f, i, j, along_x):
        _, sign, _, _ = FLOWS[f]
        peer = leaf_at(sign, 0) if along_x else leaf_at(0, sign)
        slot = (i + 1, j) if along_x else (i, j + 1)
        pltpu.make_async_remote_copy(
            source(f, i, j),
            piece(f, i, j),
            link_send,
            link_recv.at[f, slot[0], slot[1]],
            device_id={"leaf": peer},
            device_id_type=MESH,
        ).start()

    def share(f, i, j):
        pltpu.make_async_remote_copy(
            source(f, i, j),
            piece(f, i, j),
            chip_send,
            chip_recv,
            device_id={"leaf": twin},
            device_id_type=MESH,
        ).start()

    for t in range(NX + NY - 1):
        for i in range(NX):
            j = t - i
            if j < 0 or j >= NY:
                continue
            for f in range(4):
                x_first = FLOWS[f][0]
                if t > 0:
                    part = piece(f, i, j)
                    pltpu.make_async_copy(part, part, link_recv.at[f, i, j]).wait()
                if x_first:
                    if j == 0 and i < NX - 1:
                        push(f, i, j, True)
                    if j < NY - 1:
                        push(f, i, j, False)
                else:
                    if i == 0 and j < NY - 1:
                        push(f, i, j, False)
                    if i < NX - 1:
                        push(f, i, j, True)
                share(f, i, j)
        if t == 0:
            for s in range(1, NZ):
                pltpu.make_async_remote_copy(
                    coef,
                    probes.at[z],
                    z_send,
                    z_recv,
                    device_id={"probe": lax.rem(z + s, NZ)},
                    device_id_type=MESH,
                ).start()

    own.wait()
    own_coef.wait()
    half = table.at[1 - core]
    pltpu.make_async_copy(half, half, chip_recv).wait()
    half = table.at[core]
    pltpu.make_async_copy(half, half, chip_send).wait()
    sent = table.at[core, 0 : CHIPS - 1]
    pltpu.make_async_copy(sent, sent, link_send).wait()
    others = probes.at[0 : NZ - 1]
    pltpu.make_async_copy(others, others, z_recv).wait()
    pltpu.make_async_copy(others, others, z_send).wait()


def spread(payload, coef):
    dma = pltpu.SemaphoreType.DMA
    return pl.pallas_call(
        spread_kernel,
        out_shape=(
            jax.ShapeDtypeStruct((2, CHIPS, TILES, 16, 128), BF16),
            jax.ShapeDtypeStruct((NZ,) + coef.shape, BF16),
        ),
        in_specs=[pl.BlockSpec(memory_space=pl.ANY)] * 2,
        out_specs=[pl.BlockSpec(memory_space=pl.ANY)] * 2,
        scratch_shapes=[
            dma((4, NX, NY)),
            dma(()),
            dma(()),
            dma(()),
            dma(()),
            dma(()),
            dma((2,)),
        ],
        compiler_params=pltpu.CompilerParams(collective_id=0, has_side_effects=True),
        name="spread",
    )(payload, coef)


CHUNKS = 8
PER = ROWS // CHUNKS


def sweep_kernel(
    fine_slots,
    coarse_slots,
    fine_rows,
    coarse_rows,
    table,
    target_feats,
    scale,
    probes,
    transfer,
    far,
    partial,
    tiles,
    sems,
):
    z = lax.axis_index("probe")

    def fetch(n):
        return pltpu.make_async_copy(
            table.at[pl.ds(n * PER, PER)], tiles.at[pl.ds(n * PER, PER)], sems.at[n]
        )

    for n in range(CHUNKS):
        fetch(n).start()
    tiles[ZERO] = jnp.zeros((16, 128), BF16)
    tiles[SPAN + ZERO] = jnp.zeros((16, 128), BF16)
    for n in range(CHUNKS):
        fetch(n).wait()

        def swap(i, carry):
            for u in range(8):
                at = n * PER + i * 8 + u
                block = tiles[at]
                tiles[SPAN + at] = jnp.concatenate([block[:, 64:], block[:, :64]], axis=1)
            return carry

        lax.fori_loop(0, PER // 8, swap, 0)

    left_half = lax.broadcasted_iota(jnp.int32, (16, 128), 1) < 64

    def gather_pair(slots, rows, s, m):
        first = tiles[rows[0, slots[s, m]]]
        second = tiles[rows[1, slots[s, m + 1]]]
        return jnp.where(left_half, first, second)

    def one_target(slots, rows, s, feats):
        total = jnp.zeros((16, RANK), F32)
        for m in range(0, PAIRS, 4):
            both = jnp.concatenate(
                [gather_pair(slots, rows, s, m), gather_pair(slots, rows, s, m + 2)], axis=1
            )
            exponent = lax.dot_general(
                feats,
                jnp.concatenate([both, both], axis=0),
                (((1,), (0,)), ((), ())),
                preferred_element_type=F32,
            )
            weights = jnp.exp2(exponent).astype(BF16)
            total = total + lax.dot_general(both, weights, NT, preferred_element_type=F32)
        return total[8:16]

    def feats_of(t):
        return target_feats[t].astype(F32).T.astype(BF16)

    def coarse_feats(q):
        return feats_of(FT + q // 2)

    def step(q2, carry):
        coarse_pair = feats_of(FT + q2)
        for h in range(2):
            q = q2 * 2 + h
            fine_pair = feats_of(q)
            up = one_target(coarse_slots, coarse_rows, q, coarse_pair[h * 64 : h * 64 + 64])
            low = one_target(fine_slots, fine_rows, 2 * q, fine_pair[0:64])
            high = one_target(fine_slots, fine_rows, 2 * q + 1, fine_pair[64:128])
            at = pl.ds(pl.multiple_of((FT + q2) * 128, 128), 128)
            up = up * scale[:, at][:, h * 64 : h * 64 + 64]
            mats = transfer[:, pl.ds(pl.multiple_of(q * 128, 128), 128)]
            empty = jnp.zeros((8, RANK), F32)
            spread_up = jnp.concatenate(
                [
                    jnp.concatenate([up, empty], axis=1),
                    jnp.concatenate([empty, up], axis=1),
                ],
                axis=0,
            ).astype(BF16)
            down = lax.dot_general(spread_up, mats, NT, preferred_element_type=F32)
            cut = pl.ds(pl.multiple_of(q * 128, 128), 128)
            near = jnp.concatenate([low, high], axis=1) * scale[:, cut]
            far[:, cut] = near + jnp.concatenate([down[0:8], down[8:16]], axis=1)
        return carry

    lax.fori_loop(0, CT, step, 0)

    whole = far[...]
    first = whole.astype(BF16)
    rest = whole - first.astype(F32)
    second = rest.astype(BF16)
    third = (rest - second.astype(F32)).astype(BF16)
    coefs = probes[...].reshape(NZ * 8, FINE * RANK)
    gram = (
        lax.dot_general(coefs, first, NT, preferred_element_type=F32)
        + lax.dot_general(coefs, second, NT, preferred_element_type=F32)
        + lax.dot_general(coefs, third, NT, preferred_element_type=F32)
    )
    wide = jnp.concatenate([gram, jnp.zeros((NZ * 8, 120), F32)], axis=1)
    partial[...] = pltpu.roll(wide, z * 8, 1)


def sweep(fine_slots, coarse_slots, fine_rows, coarse_rows, table, feats, scale, probes, transfer):
    vm = pl.BlockSpec(memory_space=pltpu.VMEM)
    sm = pl.BlockSpec(memory_space=pltpu.SMEM)
    return pl.pallas_call(
        sweep_kernel,
        out_shape=(
            jax.ShapeDtypeStruct((8, FINE * RANK), F32),
            jax.ShapeDtypeStruct((NZ * 8, 128), F32),
        ),
        in_specs=[sm, sm, sm, sm, pl.BlockSpec(memory_space=pl.ANY), vm, vm, vm, vm],
        out_specs=[vm, vm],
        scratch_shapes=[
            pltpu.VMEM((2 * SPAN, 16, 128), BF16),
            pltpu.SemaphoreType.DMA((CHUNKS,)),
        ],
        compiler_params=pltpu.CompilerParams(vmem_limit_bytes=VMEM_LIMIT),
        name="sweep",
    )(fine_slots, coarse_slots, fine_rows, coarse_rows, table, feats, scale, probes, transfer)


def reduce_kernel(gram_scale, partial, out, at_z, at_x, at_y, work, recv, send):
    leaf = lax.axis_index("leaf")
    z = lax.axis_index("probe")
    inner = lax.rem(leaf, 2 * NX)
    y = leaf // (2 * NX)

    def z_peer(s):
        return {"probe": lax.rem(z + s, NZ)}

    def x_peer(s):
        return {"leaf": y * (2 * NX) + lax.rem(inner + s, 2 * NX)}

    def y_peer(s):
        return {"leaf": lax.rem(y + s, NY) * (2 * NX) + inner}

    barrier = pltpu.get_barrier_semaphore()
    for peer in (z_peer, x_peer, y_peer):
        for s in range(1, 8):
            pl.semaphore_signal(barrier, 1, device_id=peer(s), device_id_type=MESH)
    pl.semaphore_wait(barrier, 21)

    def exchange(stage, peer, me, source, buffer):
        for s in range(1, 8):
            pltpu.make_async_remote_copy(
                source(s),
                buffer.at[me],
                send.at[stage],
                recv.at[stage],
                device_id=peer(s),
                device_id_type=MESH,
            ).start()
        buffer[me] = source(0)[...]
        got = buffer.at[0:7]
        pltpu.make_async_copy(got, got, recv.at[stage]).wait()
        total = buffer[0]
        for n in range(1, 8):
            total = total + buffer[n]
        pltpu.make_async_copy(got, got, send.at[stage]).wait()
        return total

    work[0] = exchange(0, z_peer, z, lambda s: partial.at[lax.rem(z + s, NZ)], at_z)
    work[1] = exchange(1, x_peer, inner, lambda s: work.at[0], at_x)
    out[...] = exchange(2, y_peer, y, lambda s: work.at[1], at_y) * gram_scale


def reduce_gram(partial, gram_scale):
    vm = pl.BlockSpec(memory_space=pltpu.VMEM)
    return pl.pallas_call(
        functools.partial(reduce_kernel, gram_scale),
        out_shape=jax.ShapeDtypeStruct((8, 128), F32),
        in_specs=[vm],
        out_specs=vm,
        scratch_shapes=[
            pltpu.VMEM((8, 8, 128), F32),
            pltpu.VMEM((8, 8, 128), F32),
            pltpu.VMEM((8, 8, 128), F32),
            pltpu.VMEM((2, 8, 128), F32),
            pltpu.SemaphoreType.DMA((3,)),
            pltpu.SemaphoreType.DMA((3,)),
        ],
        compiler_params=pltpu.CompilerParams(collective_id=1, has_side_effects=True),
        name="reduce_gram",
    )(partial)


def row_tables(lists, leaf, clusters, offset):
    capacity = lists.shape[1]
    owner = jnp.arange(2 * CHIPS, dtype=jnp.int32)
    base = ((owner % 2) * CHIPS + owner // 2) * TILES + offset
    mine = (lax.rem(leaf, 2) * CHIPS + leaf // 2) * TILES + offset
    local = jnp.arange(clusters, dtype=jnp.int32)
    tile = jnp.concatenate(
        [mine + local // 2, (base[:, None] + lists // 2).reshape(2 * CHIPS * capacity)]
    )
    odd = jnp.concatenate([local % 2, (lists % 2).reshape(2 * CHIPS * capacity)])
    rows = jnp.stack([tile + odd * SPAN, tile + (1 - odd) * SPAN])
    return jnp.pad(rows, ((0, 0), (0, 1)), constant_values=ZERO)


def masked(slots, counts):
    live = lax.broadcasted_iota(jnp.int32, slots.shape, 1) < counts[:, None]
    return live


def shards(
    coef_fine,
    points_fine,
    points_coarse,
    transfer,
    send_fine,
    slots_fine,
    counts_fine,
    send_coarse,
    slots_coarse,
    counts_coarse,
):
    leaf = lax.axis_index("leaf")
    cap_fine, cap_coarse = send_fine.shape[2], send_coarse.shape[2]
    lists = jnp.concatenate(
        [send_fine[0], send_coarse[0], jnp.zeros((64, 32 - cap_fine - cap_coarse), jnp.int32)],
        axis=1,
    )
    lists = lists.astype(BF16).reshape(16, 128)
    payload, feats, scale = prep(coef_fine, points_fine, points_coarse, transfer, lists)
    table, probes = spread(payload, coef_fine)
    got = table[:, :, LIST_TILE].transpose(1, 0, 2, 3).reshape(2 * CHIPS, 64, 32)
    got = lax.dynamic_index_in_dim(got, leaf, 1, keepdims=False).astype(jnp.int32)
    fine_rows = row_tables(got[:, 0:cap_fine], leaf, FINE, 0)
    coarse_rows = row_tables(got[:, cap_fine : cap_fine + cap_coarse], leaf, COARSE, FT)
    fine_slots = jnp.where(
        masked(slots_fine, counts_fine), slots_fine, FINE + 2 * CHIPS * cap_fine
    )
    coarse_slots = jnp.where(
        masked(slots_coarse, counts_coarse), slots_coarse, COARSE + 2 * CHIPS * cap_coarse
    )
    far, partial = sweep(
        fine_slots,
        coarse_slots,
        fine_rows,
        coarse_rows,
        table.reshape(ROWS, 16, 128),
        feats,
        scale,
        probes,
        transfer,
    )
    gram_scale = 1.0 / math.sqrt(2 * CHIPS * FINE * RANK)
    gram = reduce_gram(partial.reshape(NZ, 8, 128), gram_scale)
    return (far, gram[:, 0 : NZ * 8])


def solution(mesh):
    return jax.shard_map(
        shards,
        mesh=mesh,
        in_specs=(
            P("probe", "leaf"),
            P(None, "leaf"),
            P(None, "leaf"),
            P(None, "leaf"),
            P("leaf", None, None),
            P("leaf", None),
            P("leaf"),
            P("leaf", None, None),
            P("leaf", None),
            P("leaf"),
        ),
        out_specs=(P("probe", "leaf"), P("probe", None)),
        check_vma=False,
    )
```

time: 575 us -> 166 us (0.29); the launches traced: 564 us -> 166 us
  Pallas kernels: 0 us -> 155 us
  local copies, waits for them, and re-layouts: 152 us -> 5.11 us
  blocking collectives: 129 us -> 0 us
  matrix products: 121 us -> 0 us
  waiting for transfers between devices: 58 us -> 0 us
  other arithmetic: 54.3 us -> 4.84 us
  starting transfers between devices: 33.6 us -> 0 us
  between operations: 14.6 us -> 0.76 us
    pallas_call x0 -> x4, Pallas kernels: none -> 155 us  [the longest x1 73.2 us: sweep(): pl.pallas_call(sweep_kernel, out_shape=(jax.ShapeDtypeStruct((8, FINE * R...]
    psum x1 -> x0, blocking collectives: 129 us -> none  [shards(): probe_gram = lax.psum(partial_gram, 'leaf') * gram_scale]
    dot_general x27 -> x0, matrix products: 121 us -> none  [the longest x24 116 us: one_group(): jnp.einsum('gmkj,gmpj->gpk', weights, partner_coef, preferred_element_typ...]
    gather x52 -> x0, local copies, waits for them, and re-layouts: 84.6 us -> none  [the longest x24 45.7 us: one_group(): partner_coef = table_coef[slot_group]]
    all_gather x1 -> x0, waiting for transfers between devices: 41.6 us -> none  [shards(): lax.all_gather(far_field, 'probe', axis=0, tiled=True)]
    all_to_all x4 -> x0, starting transfers between devices: 33.6 us -> none  [the longest x1 11.8 us: shards(): lax.all_to_all(coarse_point_pack, 'leaf', split_axis=0, concat_axis=0, ti...]
    all_to_all x6 -> x0, other arithmetic: 28.6 us -> none  [the longest x2 16 us: shards(): lax.all_to_all(fine_coef_pack, 'leaf', split_axis=0, concat_axis=0, tiled...]
    squeeze x24 -> x0, local copies, waits for them, and re-layouts: 16.8 us -> none  [level_sweep(): lax.map(one_group, (slot_table.reshape(turns, group_size, pair_slots), co...]
  transfers between devices with their start and end apart: 5 -> 0, of which waited for: 3 -> 0; matrix products, arithmetic and copies ran while one was open for 22% -> 0% of each run, Pallas kernels for 0% -> 0%
where the time goes in v1:
time: 166 us
  Pallas kernels  155 us (93%)
  local copies, waits for them, and re-layouts  5.11 us (3%)
  other arithmetic  4.84 us (3%)
    pallas_call x1, Pallas kernels, sweep(): pl.pallas_call(sweep_kernel, out_shape=(jax.ShapeDtypeStruct((8, FINE * R...  73.2 us
    pallas_call x1, Pallas kernels, spread(): pl.pallas_call(spread_kernel, out_shape=(jax.ShapeDtypeStruct((2, CHIPS,...  61.5 us
    pallas_call x1, Pallas kernels, reduce_gram(): pl.pallas_call(functools.partial(reduce_kernel, gram_scale), out_shape=ja...  17.7 us

profile of v1, /device:TPU:1, one launch (start us, length us, event | category | flops | bytes accessed | tf_op | source)
XLA Modules:
  0.0 165.6 jit_solution(5132601471286675683)
XLA Ops:
  0.7 0.7 convert_bitcast_fusion
  1.4 0.7 convert_bitcast_fusion.1
  2.1 0.1 pad.24.clone
  2.1 0.1 maximum_maximum_fusion
  2.2 0.1 copy.13
  2.3 0.7 convert_element_type.11.lists
  3.0 2.6 %prep.1 = (bf16[49,16,128]{2,1,0:T(8,128)(2,1)}, bf16[48,32,128]{2,1,0:T(8,128)(2,1)}, f32[8,6144]{1,0:T(8,128)}) custom-call(bf16[8,4096]{1,0:T(8,128)(2,1)} %coef.3, f32[3,4096]{1,0:T(4,128)} %fine_pts.1, f32[3,2048]{1,0:T(4,128)} %coarse_pts.1, bf16[64,4096]{1,0:T(8,128)(2,1)} %transfer.3, bf16[16,128]{1,0:T(8,128)(2,1)} %convert_element_type.11.lists), custom_call_target="tpu_custom_call" | custom-call | tf_op jit(solution)/shard_map/prep/pallas_call | solution.py:89
  5.6 61.5 %spread.1 = (bf16[2,32,49,16,128]{4,3,2,1,0:T(8,128)(2,1)}, bf16[8,8,4096]{2,1,0:T(8,128)(2,1)}) custom-call(bf16[49,16,128]{2,1,0:T(8,128)(2,1)} %get-tuple-element.9.payload, bf16[8,4096]{1,0:T(8,128)(2,1)} %coef.3), custom_call_target="tpu_custom_call" | custom-call | tf_op jit(solution)/shard_map/spread/pallas_call | solution.py:219
  67.1 1.0 slice_bitcast_fusion
  68.1 0.4 reshape.264
  68.5 0.1 dynamic-slice_convert_fusion
  68.6 0.1 fusion.1
  68.7 0.1 add_select_fusion
  68.8 0.1 concatenate.99
  68.8 0.1 concatenate.96
  68.9 0.1 multiply_add_fusion.3
  69.0 0.6 pad.9.coarse_rows
  69.6 0.1 fusion
  69.7 0.1 concatenate.93
  69.8 0.1 concatenate.90
  69.9 0.1 multiply_add_fusion.1
  70.0 0.6 pad.8.fine_rows
  70.6 1.4 fusion.2.fine_slots
  72.1 1.4 fusion.7.coarse_slots
  73.5 73.2 %sweep.1 = (f32[8,4096]{1,0:T(8,128)}, f32[64,128]{1,0:T(8,128)}) custom-call(s32[64,64]{1,0:T(8,128)} %fusion.2.fine_slots, s32[32,64]{1,0:T(8,128)} %fusion.7.coarse_slots, s32[2,1089]{1,0:T(2,128)} %pad.8.fine_rows, s32[2,545]{1,0:T(2,128)} %pad.9.coarse_rows, bf16[3136,16,128]{2,1,0:T(8,128)(2,1)} %bitcast.22, ...), custom_call_target="tpu_custom_call" | custom-call | tf_op jit(solution)/shard_map/sweep/pallas_call | solution.py:357
  146.6 17.7 %reduce_gram.1 = f32[8,128]{1,0:T(8,128)} custom-call(f32[8,8,128]{2,1,0:T(8,128)} %bitcast.27), custom_call_target="tpu_custom_call" | custom-call | tf_op jit(solution)/shard_map/reduce_gram/pallas_call | solution.py:421
  164.3 1.3 copy.16
  (9 shorter events, 0.1 us)

commit v2 on v1

--- a/solution.py
+++ b/solution.py
@@ -15,15 +15,18 @@
 CHIPS = NX * NY
 FINE, COARSE, PAIRS = 64, 32, 64
 FT, CT = FINE // 2, COARSE // 2
-TILES = FT + CT + 1
-LIST_TILE = FT + CT
+HALF = FT + CT
+TILES = HALF + 2
 ROWS = 2 * CHIPS * TILES
-ZERO = ROWS
 SPAN = ROWS + 8
 MESH = pl.DeviceIdType.MESH
 F32, BF16 = jnp.float32, jnp.bfloat16
+BATCH, LAG = 1, 12
+UNROLL = 2
 NT = (((1,), (1,)), ((), ()))
-VMEM_LIMIT = 60 * 1024 * 1024
+TABLE_SPACE = pltpu.VMEM
+SPREAD_LIMIT = 20 * 1024 * 1024
+SWEEP_LIMIT = 24 * 1024 * 1024
 
 
 def features(points):
@@ -49,23 +52,21 @@
             scaled_low,
             nothing[0:2],
             nothing,
+            bias,
+            nothing[0:7],
         ],
         axis=0,
     )
-    return source, target, jnp.exp(squares * -kernel_rate)
-
-
-def prep_kernel(coef, fine_pts, coarse_pts, transfer, lists, payload, target_out, scale_out):
-    source, target, scale = features(fine_pts[...])
-    rows = jnp.concatenate([source, coef[...].astype(F32)], axis=0).astype(BF16)
-    target = target.astype(BF16)
+    return source, target
+
+
+def prep_kernel(coef, fine_pts, coarse_pts, transfer, fine_list, coarse_list, payload, target_out):
+    source, target = features(fine_pts[...])
     for t in range(FT):
         cut = slice(t * 128, t * 128 + 128)
-        payload[t] = rows[:, cut]
+        payload[t] = jnp.concatenate([source[:, cut], coef[:, cut].astype(F32)], axis=0).astype(BF16)
         target_out[t] = target[:, cut]
-    scale_out[:, 0 : FT * 128] = jnp.broadcast_to(scale, (8, FT * 128))
-    source, target, scale = features(coarse_pts[...])
-    target = target.astype(BF16)
+    source, target = features(coarse_pts[...])
     for t in range(CT):
         halves = []
         for q in (2 * t, 2 * t + 1):
@@ -81,33 +82,34 @@
         rows = jnp.concatenate([source[:, cut], jnp.concatenate(halves, axis=1)], axis=0)
         payload[FT + t] = rows.astype(BF16)
         target_out[FT + t] = target[:, cut]
-    scale_out[:, FT * 128 :] = jnp.broadcast_to(scale, (8, CT * 128))
-    payload[LIST_TILE] = lists[...]
-
-
-def prep(coef, fine_pts, coarse_pts, transfer, lists):
+    entries = [fine_list[...].astype(F32), coarse_list[...].astype(F32), jnp.zeros((8, 64), F32)]
+    for n in range(2):
+        part = entries[0] if n == 0 else jnp.concatenate(entries[1:], axis=0)
+        payload[HALF + n] = jnp.concatenate([part, jnp.zeros((16, 64), F32)], axis=1).astype(BF16)
+
+
+def prep(coef, fine_pts, coarse_pts, transfer, fine_list, coarse_list):
     return pl.pallas_call(
         prep_kernel,
         out_shape=(
             jax.ShapeDtypeStruct((TILES, 16, 128), BF16),
-            jax.ShapeDtypeStruct((FT + CT, 32, 128), BF16),
-            jax.ShapeDtypeStruct((8, (FT + CT) * 128), F32),
+            jax.ShapeDtypeStruct((HALF, 40, 128), F32),
         ),
-        compiler_params=pltpu.CompilerParams(vmem_limit_bytes=VMEM_LIMIT),
+        compiler_params=pltpu.CompilerParams(vmem_limit_bytes=8 * 1024 * 1024),
         name="prep",
-    )(coef, fine_pts, coarse_pts, transfer, lists)
+    )(coef, fine_pts, coarse_pts, transfer, fine_list, coarse_list)
 
 
 FLOWS = (
     (True, 1, 0, 10),
     (True, -1, 10, 20),
     (False, 1, 20, 35),
-    (False, -1, 35, 49),
+    (False, -1, 35, 50),
 )
 
 
 def spread_kernel(
-    payload, coef, table, probes, link_recv, link_send, chip_recv, chip_send, z_recv, z_send, own_sem
+    payload, coef, table, probes, zeros, link_recv, link_send, chip_recv, chip_send, z_recv, z_send, own_sem
 ):
     leaf = lax.axis_index("leaf")
     z = lax.axis_index("probe")
@@ -133,14 +135,20 @@
         )
     pl.semaphore_wait(barrier, len(peers) + NZ - 1)
 
-    own = pltpu.make_async_copy(payload, table.at[core, chip], own_sem.at[0])
+    def rows_of(which_chip, low, high):
+        return table.at[pl.ds((core * CHIPS + which_chip) * TILES + low, high - low)]
+
+    zeros[...] = jnp.zeros_like(zeros)
+    own = pltpu.make_async_copy(payload, rows_of(chip, 0, TILES), own_sem.at[0])
     own.start()
+    clear = pltpu.make_async_copy(zeros, table.at[ROWS:SPAN], own_sem.at[2])
+    clear.start()
     own_coef = pltpu.make_async_copy(coef, probes.at[z], own_sem.at[1])
     own_coef.start()
 
     def piece(f, i, j):
         _, sign, low, high = FLOWS[f]
-        return table.at[core, chip_at(-sign * i, -sign * j), low:high]
+        return rows_of(chip_at(-sign * i, -sign * j), low, high)
 
     def source(f, i, j):
         _, _, low, high = FLOWS[f]
@@ -203,11 +211,11 @@
 
     own.wait()
     own_coef.wait()
-    half = table.at[1 - core]
+    clear.wait()
+    half = table.at[0 : ROWS // 2]
     pltpu.make_async_copy(half, half, chip_recv).wait()
-    half = table.at[core]
     pltpu.make_async_copy(half, half, chip_send).wait()
-    sent = table.at[core, 0 : CHIPS - 1]
+    sent = table.at[0 : (CHIPS - 1) * TILES]
     pltpu.make_async_copy(sent, sent, link_send).wait()
     others = probes.at[0 : NZ - 1]
     pltpu.make_async_copy(others, others, z_recv).wait()
@@ -219,107 +227,157 @@
     return pl.pallas_call(
         spread_kernel,
         out_shape=(
-            jax.ShapeDtypeStruct((2, CHIPS, TILES, 16, 128), BF16),
+            jax.ShapeDtypeStruct((SPAN, 16, 128), BF16),
             jax.ShapeDtypeStruct((NZ,) + coef.shape, BF16),
         ),
         in_specs=[pl.BlockSpec(memory_space=pl.ANY)] * 2,
-        out_specs=[pl.BlockSpec(memory_space=pl.ANY)] * 2,
+        out_specs=[pl.BlockSpec(memory_space=TABLE_SPACE), pl.BlockSpec(memory_space=TABLE_SPACE)],
         scratch_shapes=[
+            pltpu.VMEM((SPAN - ROWS, 16, 128), BF16),
             dma((4, NX, NY)),
             dma(()),
             dma(()),
             dma(()),
             dma(()),
             dma(()),
-            dma((2,)),
+            dma((3,)),
         ],
-        compiler_params=pltpu.CompilerParams(collective_id=0, has_side_effects=True),
+        compiler_params=pltpu.CompilerParams(
+            collective_id=0, has_side_effects=True, vmem_limit_bytes=SPREAD_LIMIT
+        ),
         name="spread",
     )(payload, coef)
 
 
-CHUNKS = 8
-PER = ROWS // CHUNKS
+def take(row, index):
+    return jnp.take_along_axis(jnp.broadcast_to(row, index.shape), index, axis=1)
+
+
+def slot_rows(lists, slots, counts, clusters, capacity, offset, mine):
+    rows = slots.shape[0]
+    v = jnp.concatenate([slots, jnp.zeros((rows, 128 - PAIRS), jnp.int32)], axis=1)
+    remote = jnp.maximum(v - clusters, 0)
+    owner = remote // capacity
+    entry = remote - owner * capacity
+    found = jnp.zeros((rows, 128), jnp.int32)
+    for i in range(capacity):
+        found = jnp.where(entry == i, take(lists[i : i + 1], owner), found)
+    is_own = v < clusters
+    cluster = jnp.where(is_own, v, found)
+    base = jnp.where(is_own, mine, ((owner % 2) * CHIPS + owner // 2) * TILES)
+    row = base + offset + cluster // 2
+    spot = lax.broadcasted_iota(jnp.int32, (rows, 128), 1)
+    wide = jnp.broadcast_to(counts.astype(F32), (128, rows)).T
+    live = spot.astype(F32) < wide
+    row = jnp.where(live, row, ROWS)
+    turn = ((cluster + spot) % 2) * 64
+    return row, turn
 
 
 def sweep_kernel(
     fine_slots,
     coarse_slots,
-    fine_rows,
-    coarse_rows,
-    table,
+    fine_counts,
+    coarse_counts,
+    tiles,
     target_feats,
-    scale,
     probes,
     transfer,
     far,
     partial,
-    tiles,
-    sems,
+    stage0,
+    stage1,
+    staged,
+    picks,
+    sem,
 ):
     z = lax.axis_index("probe")
-
-    def fetch(n):
-        return pltpu.make_async_copy(
-            table.at[pl.ds(n * PER, PER)], tiles.at[pl.ds(n * PER, PER)], sems.at[n]
-        )
-
-    for n in range(CHUNKS):
-        fetch(n).start()
-    tiles[ZERO] = jnp.zeros((16, 128), BF16)
-    tiles[SPAN + ZERO] = jnp.zeros((16, 128), BF16)
-    for n in range(CHUNKS):
-        fetch(n).wait()
-
-        def swap(i, carry):
-            for u in range(8):
-                at = n * PER + i * 8 + u
-                block = tiles[at]
-                tiles[SPAN + at] = jnp.concatenate([block[:, 64:], block[:, :64]], axis=1)
-            return carry
-
-        lax.fori_loop(0, PER // 8, swap, 0)
-
-    left_half = lax.broadcasted_iota(jnp.int32, (16, 128), 1) < 64
-
-    def gather_pair(slots, rows, s, m):
-        first = tiles[rows[0, slots[s, m]]]
-        second = tiles[rows[1, slots[s, m + 1]]]
-        return jnp.where(left_half, first, second)
-
-    def one_target(slots, rows, s, feats):
-        total = jnp.zeros((16, RANK), F32)
-        for m in range(0, PAIRS, 4):
-            both = jnp.concatenate(
-                [gather_pair(slots, rows, s, m), gather_pair(slots, rows, s, m + 2)], axis=1
-            )
-            exponent = lax.dot_general(
-                feats,
-                jnp.concatenate([both, both], axis=0),
-                (((1,), (0,)), ((), ())),
-                preferred_element_type=F32,
-            )
-            weights = jnp.exp2(exponent).astype(BF16)
-            total = total + lax.dot_general(both, weights, NT, preferred_element_type=F32)
-        return total[8:16]
+    leaf = lax.axis_index("leaf")
+    mine = ((leaf % 2) * CHIPS + leaf // 2) * TILES
+
+    lane = lax.broadcasted_iota(jnp.int32, (16, 128), 1)
+    lists = [jnp.zeros((16, 128), F32) for _ in range(2)]
+    for e in range(2 * CHIPS):
+        base = ((e % 2) * CHIPS + e // 2) * TILES + HALF
+        for n in range(2):
+            got = pltpu.roll(tiles[base + n].astype(F32), lax.rem(e - leaf + 128, 128), 1)
+            lists[n] = jnp.where(lane == e, got, lists[n])
+    lists = [part.astype(jnp.int32) for part in lists]
+    row, turn = slot_rows(lists[0], fine_slots[...], fine_counts[...], FINE, 16, 0, mine)
+    staged[0:FINE] = row
+    staged[FINE + COARSE : 2 * FINE + COARSE] = turn
+    row, turn = slot_rows(
+        lists[1], coarse_slots[...], coarse_counts[...], COARSE, 8, FT, mine
+    )
+    staged[FINE : FINE + COARSE] = row
+    staged[2 * FINE + COARSE :] = turn
+    move = pltpu.make_async_copy(staged, picks, sem)
+    move.start()
+    move.wait()
+
+    left_half = lane < 64
+    stage = (stage0, stage1)
+
+    def gather_pair(s, p, into):
+        m = 2 * p
+        first = pltpu.roll(tiles[picks[s, m]], picks[FINE + COARSE + s, m], 1)
+        second = pltpu.roll(tiles[picks[s, m + 1]], picks[FINE + COARSE + s, m + 1], 1)
+        into[p] = jnp.where(left_half, first, second)
 
     def feats_of(t):
-        return target_feats[t].astype(F32).T.astype(BF16)
-
-    def coarse_feats(q):
-        return feats_of(FT + q // 2)
-
-    def step(q2, carry):
-        coarse_pair = feats_of(FT + q2)
-        for h in range(2):
-            q = q2 * 2 + h
-            fine_pair = feats_of(q)
-            up = one_target(coarse_slots, coarse_rows, q, coarse_pair[h * 64 : h * 64 + 64])
-            low = one_target(fine_slots, fine_rows, 2 * q, fine_pair[0:64])
-            high = one_target(fine_slots, fine_rows, 2 * q + 1, fine_pair[64:128])
-            at = pl.ds(pl.multiple_of((FT + q2) * 128, 128), 128)
-            up = up * scale[:, at][:, h * 64 : h * 64 + 64]
-            mats = transfer[:, pl.ds(pl.multiple_of(q * 128, 128), 128)]
+        block = target_feats[t].T
+        return block[:, 0:32].astype(BF16), block[:, 32:33]
+
+    for p in range(PAIRS // 2):
+        gather_pair(FINE, p, stage0)
+
+    def step(base, carry):
+        order, packs, sides = [], [], []
+        for u in range(UNROLL):
+            t = base * UNROLL + u
+            order += [FINE + 2 * t, 4 * t, 4 * t + 1, FINE + 2 * t + 1, 4 * t + 2, 4 * t + 3]
+            packs += [feats_of(FT + t), feats_of(2 * t), feats_of(2 * t + 1)]
+            n = 3 * u
+            sides += [(n, 0), (n + 1, 0), (n + 1, 1), (n, 1), (n + 2, 0), (n + 2, 1)]
+        order.append(FINE + 2 * jnp.minimum((base + 1) * UNROLL, CT - 1))
+        totals = [None for _ in range(6 * UNROLL)]
+        waiting = []
+
+        def flush():
+            for r, both, weights in waiting.pop(0):
+                part = lax.dot_general(both, weights, NT, preferred_element_type=F32)
+                totals[r] = part[8:16] if totals[r] is None else totals[r] + part[8:16]
+
+        for r in range(6 * UNROLL):
+            pack, half = sides[r]
+            cut = slice(half * 64, half * 64 + 64)
+            feats, bias = packs[pack][0][cut], packs[pack][1][cut]
+            source = stage[r % 2]
+            for group in range(PAIRS // (4 * BATCH)):
+                batch = []
+                for n in range(BATCH):
+                    p = group * 2 * BATCH + n * 2
+                    both = jnp.concatenate([source[p], source[p + 1]], axis=1)
+                    exponent = lax.dot_general(
+                        feats,
+                        jnp.concatenate([both, both], axis=0),
+                        (((1,), (0,)), ((), ())),
+                        preferred_element_type=F32,
+                    )
+                    batch.append((r, both, jnp.exp2(exponent + bias).astype(BF16)))
+                waiting.append(batch)
+                if len(waiting) > LAG:
+                    flush()
+                for n in range(2 * BATCH):
+                    gather_pair(order[r + 1], group * 2 * BATCH + n, stage[(r + 1) % 2])
+        while waiting:
+            flush()
+        outs = totals
+        for h in range(2 * UNROLL):
+            q = base * 2 * UNROLL + h
+            up, low, high = outs[3 * h : 3 * h + 3]
+            cut = pl.ds(pl.multiple_of(q * 128, 128), 128)
+            mats = transfer[:, cut]
             empty = jnp.zeros((8, RANK), F32)
             spread_up = jnp.concatenate(
                 [
@@ -329,12 +387,10 @@
                 axis=0,
             ).astype(BF16)
             down = lax.dot_general(spread_up, mats, NT, preferred_element_type=F32)
-            cut = pl.ds(pl.multiple_of(q * 128, 128), 128)
-            near = jnp.concatenate([low, high], axis=1) * scale[:, cut]
-            far[:, cut] = near + jnp.concatenate([down[0:8], down[8:16]], axis=1)
+            far[:, cut] = jnp.concatenate([low + down[0:8], high + down[8:16]], axis=1)
         return carry
 
-    lax.fori_loop(0, CT, step, 0)
+    lax.fori_loop(0, CT // UNROLL, step, 0)
 
     whole = far[...]
     first = whole.astype(BF16)
@@ -351,24 +407,26 @@
     partial[...] = pltpu.roll(wide, z * 8, 1)
 
 
-def sweep(fine_slots, coarse_slots, fine_rows, coarse_rows, table, feats, scale, probes, transfer):
+def sweep(fine_slots, coarse_slots, fine_counts, coarse_counts, table, feats, probes, transfer):
     vm = pl.BlockSpec(memory_space=pltpu.VMEM)
-    sm = pl.BlockSpec(memory_space=pltpu.SMEM)
     return pl.pallas_call(
         sweep_kernel,
         out_shape=(
             jax.ShapeDtypeStruct((8, FINE * RANK), F32),
             jax.ShapeDtypeStruct((NZ * 8, 128), F32),
         ),
-        in_specs=[sm, sm, sm, sm, pl.BlockSpec(memory_space=pl.ANY), vm, vm, vm, vm],
+        in_specs=[vm] * 8,
         out_specs=[vm, vm],
         scratch_shapes=[
-            pltpu.VMEM((2 * SPAN, 16, 128), BF16),
-            pltpu.SemaphoreType.DMA((CHUNKS,)),
+            pltpu.VMEM((PAIRS // 2, 16, 128), BF16),
+            pltpu.VMEM((PAIRS // 2, 16, 128), BF16),
+            pltpu.VMEM((2 * (FINE + COARSE), 128), jnp.int32),
+            pltpu.SMEM((2 * (FINE + COARSE), 128), jnp.int32),
+            pltpu.SemaphoreType.DMA(()),
         ],
-        compiler_params=pltpu.CompilerParams(vmem_limit_bytes=VMEM_LIMIT),
+        compiler_params=pltpu.CompilerParams(vmem_limit_bytes=SWEEP_LIMIT),
         name="sweep",
-    )(fine_slots, coarse_slots, fine_rows, coarse_rows, table, feats, scale, probes, transfer)
+    )(fine_slots, coarse_slots, fine_counts, coarse_counts, table, feats, probes, transfer)
 
 
 def reduce_kernel(gram_scale, partial, out, at_z, at_x, at_y, work, recv, send):
@@ -436,25 +494,6 @@
     )(partial)
 
 
-def row_tables(lists, leaf, clusters, offset):
-    capacity = lists.shape[1]
-    owner = jnp.arange(2 * CHIPS, dtype=jnp.int32)
-    base = ((owner % 2) * CHIPS + owner // 2) * TILES + offset
-    mine = (lax.rem(leaf, 2) * CHIPS + leaf // 2) * TILES + offset
-    local = jnp.arange(clusters, dtype=jnp.int32)
-    tile = jnp.concatenate(
-        [mine + local // 2, (base[:, None] + lists // 2).reshape(2 * CHIPS * capacity)]
-    )
-    odd = jnp.concatenate([local % 2, (lists % 2).reshape(2 * CHIPS * capacity)])
-    rows = jnp.stack([tile + odd * SPAN, tile + (1 - odd) * SPAN])
-    return jnp.pad(rows, ((0, 0), (0, 1)), constant_values=ZERO)
-
-
-def masked(slots, counts):
-    live = lax.broadcasted_iota(jnp.int32, slots.shape, 1) < counts[:, None]
-    return live
-
-
 def shards(
     coef_fine,
     points_fine,
@@ -467,33 +506,17 @@
     slots_coarse,
     counts_coarse,
 ):
-    leaf = lax.axis_index("leaf")
-    cap_fine, cap_coarse = send_fine.shape[2], send_coarse.shape[2]
-    lists = jnp.concatenate(
-        [send_fine[0], send_coarse[0], jnp.zeros((64, 32 - cap_fine - cap_coarse), jnp.int32)],
-        axis=1,
+    payload, feats = prep(
+        coef_fine, points_fine, points_coarse, transfer, send_fine[0].T, send_coarse[0].T
     )
-    lists = lists.astype(BF16).reshape(16, 128)
-    payload, feats, scale = prep(coef_fine, points_fine, points_coarse, transfer, lists)
     table, probes = spread(payload, coef_fine)
-    got = table[:, :, LIST_TILE].transpose(1, 0, 2, 3).reshape(2 * CHIPS, 64, 32)
-    got = lax.dynamic_index_in_dim(got, leaf, 1, keepdims=False).astype(jnp.int32)
-    fine_rows = row_tables(got[:, 0:cap_fine], leaf, FINE, 0)
-    coarse_rows = row_tables(got[:, cap_fine : cap_fine + cap_coarse], leaf, COARSE, FT)
-    fine_slots = jnp.where(
-        masked(slots_fine, counts_fine), slots_fine, FINE + 2 * CHIPS * cap_fine
-    )
-    coarse_slots = jnp.where(
-        masked(slots_coarse, counts_coarse), slots_coarse, COARSE + 2 * CHIPS * cap_coarse
-    )
     far, partial = sweep(
-        fine_slots,
-        coarse_slots,
-        fine_rows,
-        coarse_rows,
-        table.reshape(ROWS, 16, 128),
+        slots_fine,
+        slots_coarse,
+        counts_fine.reshape(1, FINE),
+        counts_coarse.reshape(1, COARSE),
+        table,
         feats,
-        scale,
         probes,
         transfer,
     )

time: 166 us -> 124 us (0.75)
  Pallas kernels: 155 us -> 111 us
  local copies, waits for them, and re-layouts: 5.11 us -> 11.4 us
  other arithmetic: 4.84 us -> 0 us
    pallas_call x1, Pallas kernels: 73.2 us -> 32.8 us  [sweep(): pl.pallas_call(sweep_kernel, out_shape=(jax.ShapeDtypeStruct((8, FINE * R...]
    unnamed x1 -> x27, local copies, waits for them, and re-layouts: 1.28 us -> 11.4 us
    select_n x4 -> x0, other arithmetic: 2.93 us -> none  [the longest x1 1.44 us: shards(): jnp.where(masked(slots_fine, counts_fine), slots_fine, FINE + 2 * CHIPS *...]
    pallas_call x1, Pallas kernels: 2.57 us -> 0.7 us  [prep(): pl.pallas_call(prep_kernel, out_shape=(jax.ShapeDtypeStruct((TILES, 16, 1...]
where the time goes in v2:
time: 124 us; the launch traced here: 123 us
  Pallas kernels  111 us (90%)
  local copies, waits for them, and re-layouts  11.4 us (9%)
    pallas_call x1, Pallas kernels, spread(): pl.pallas_call(spread_kernel, out_shape=(jax.ShapeDtypeStruct((SPAN, 16,...  60.1 us
    pallas_call x1, Pallas kernels, sweep(): pl.pallas_call(sweep_kernel, out_shape=(jax.ShapeDtypeStruct((8, FINE * R...  32.8 us
    pallas_call x1, Pallas kernels, reduce_gram(): pl.pallas_call(functools.partial(reduce_kernel, gram_scale), out_shape=ja...  17.3 us
    unnamed x27, local copies, waits for them, and re-layouts  11.4 us

profile of v2, /device:TPU:1, one launch (start us, length us, event | category | flops | bytes accessed | tf_op | source)
XLA Modules:
  0.0 123.1 jit_solution(14459037245433010660)
XLA Ops:
  0.6 0.0 copy-start
  0.6 1.0 copy-done
  1.7 0.0 copy-start.2
  1.7 0.8 copy-done.2
  2.5 0.0 copy-start.4
  2.5 0.8 copy-done.4
  3.4 0.0 copy-start.6
  3.4 0.8 copy-done.6
  4.1 0.0 copy-start.9
  4.1 0.7 copy-done.9
  4.8 0.0 copy-start.10
  4.8 0.7 copy-done.10
  5.5 0.7 prep.1
  6.2 0.0 copy-start.3
  6.2 0.8 copy-done.3
  7.1 60.1 %spread.1 = (bf16[3208,16,128]{2,1,0:T(8,128)(2,1)S(1)}, bf16[8,8,4096]{2,1,0:T(8,128)(2,1)S(1)}) custom-call(bf16[50,16,128]{2,1,0:T(8,128)(2,1)S(1)} %get-tuple-element.8.payload, bf16[8,4096]{1,0:T(8,128)(2,1)S(1)} %copy-done.3), custom_call_target="tpu_custom_call" | custom-call | tf_op jit(solution)/shard_map/spread/pallas_call | solution.py:227
  67.2 0.0 copy-start.1
  67.2 1.0 copy-done.1
  68.2 0.0 copy-start.5
  68.2 0.8 copy-done.5
  69.0 0.0 copy-start.8
  69.0 0.7 copy-done.8
  69.7 0.0 copy-start.11
  69.7 0.7 copy-done.11
  70.4 0.0 copy-start.12
  70.4 0.7 copy-done.12
  71.0 32.8 %sweep.1 = (f32[8,4096]{1,0:T(8,128)}, f32[64,128]{1,0:T(8,128)S(1)}) custom-call(s32[64,64]{1,0:T(8,128)S(1)} %copy-done.5, s32[32,64]{1,0:T(8,128)S(1)} %copy-done.8, s32[1,64]{1,0:T(1,128)S(1)} %bitcast.13, s32[1,32]{1,0:T(1,128)S(1)} %bitcast.14, bf16[3208,16,128]{2,1,0:T(8,128)(2,1)S(1)} %get-tuple-element.9.tiles, ...), custom_call_target="tpu_custom_call" | custom-call | tf_op jit(solution)/shard_map/sweep/pallas_call | solution.py:412
  103.9 0.0 copy-start.7
  103.9 0.6 copy-done.7
  104.5 17.3 %reduce_gram.1 = f32[8,128]{1,0:T(8,128)} custom-call(f32[8,8,128]{2,1,0:T(8,128)} %bitcast.10), custom_call_target="tpu_custom_call" | custom-call | tf_op jit(solution)/shard_map/reduce_gram/pallas_call | solution.py:479
  121.8 1.3 %copy.13 = f32[8,64]{1,0:T(8,128)} copy(f32[8,64]{1,0:T(8,128)} %bitcast.15) | data formatting | bytes 4096
Async XLA Ops:
  0.6 1.0 copy-start
  1.7 0.8 copy-start.2
  2.5 0.8 copy-start.4
  3.4 0.8 copy-start.6
  4.1 0.7 copy-start.9
  4.8 0.7 copy-start.10
  6.2 0.8 copy-start.3
  67.2 1.0 copy-start.1
  68.2 0.8 copy-start.5
  69.0 0.7 copy-start.8
  69.7 0.7 copy-start.11
  70.4 0.7 copy-start.12
  103.9 0.6 copy-start.7

commit v3 on v2

v3 whole, which is shorter than its diff:
```python
import functools
import math

import jax
import jax.numpy as jnp
from jax import lax
from jax.experimental import pallas as pl
from jax.experimental.pallas import tpu as pltpu
from jax.sharding import PartitionSpec as P

kernel_rate = 1.5
LOG2E = 1.4426950408889634
RANK = 64
NX, NY, NZ = 4, 8, 8
CHIPS = NX * NY
FINE, COARSE, PAIRS = 64, 32, 64
FT, CT = FINE // 2, COARSE // 2
HALF = FT + CT
SIZES = (CT + 2, FT)
ENDS = (2 * CHIPS * SIZES[0], 2 * CHIPS * SIZES[1])
PAD = 8
MESH = pl.DeviceIdType.MESH
F32, BF16 = jnp.float32, jnp.bfloat16
LAG = 12
LEAD = 2
EACH = 16
NT = (((1,), (1,)), ((), ()))
TABLE_SPACE = pltpu.VMEM
SPREAD_LIMIT = 20 * 1024 * 1024
SWEEP_LIMIT = 24 * 1024 * 1024


def features(points):
    high = points.astype(BF16).astype(F32)
    low = (points - high).astype(BF16).astype(F32)
    squares = points[0:1] * points[0:1] + points[1:2] * points[1:2] + points[2:3] * points[2:3]
    bias = squares * (-kernel_rate * LOG2E)
    bias_high = bias.astype(BF16).astype(F32)
    bias_low = (bias - bias_high).astype(BF16).astype(F32)
    scaled = points * (2.0 * kernel_rate * LOG2E)
    scaled_high = scaled.astype(BF16).astype(F32)
    scaled_low = (scaled - scaled_high).astype(BF16).astype(F32)
    ones = jnp.ones((2, points.shape[1]), F32)
    nothing = jnp.zeros((8, points.shape[1]), F32)
    source = jnp.concatenate([high, low, bias_high, bias_low], axis=0)
    target = jnp.concatenate(
        [
            scaled_high,
            scaled_high,
            ones,
            nothing,
            scaled_low,
            scaled_low,
            nothing[0:2],
            nothing,
            bias,
            nothing[0:7],
        ],
        axis=0,
    )
    return source, target


def prep_kernel(
    coef_in,
    fine_pts_in,
    coarse_pts_in,
    transfer_in,
    fine_list_in,
    coarse_list_in,
    fine_slots_in,
    coarse_slots_in,
    fine_counts_in,
    coarse_counts_in,
    coarse_payload,
    fine_payload,
    target_out,
    codes,
    coef,
    transfer,
    fine_pts,
    coarse_pts,
    fine_list,
    coarse_list,
    fine_slots,
    coarse_slots,
    fine_counts,
    coarse_counts,
    sems,
):
    moves = [
        (fine_pts_in, fine_pts),
        (coef_in, coef),
        (transfer_in, transfer),
        (coarse_pts_in, coarse_pts),
        (fine_list_in, fine_list),
        (coarse_list_in, coarse_list),
        (fine_slots_in, fine_slots),
        (coarse_slots_in, coarse_slots),
        (fine_counts_in, fine_counts),
        (coarse_counts_in, coarse_counts),
    ]
    copies = [pltpu.make_async_copy(a, b, sems.at[n]) for n, (a, b) in enumerate(moves)]
    for copy in copies:
        copy.start()
    copies[0].wait()
    copies[1].wait()
    source, target = features(fine_pts[...])
    for t in range(FT):
        cut = slice(t * 128, t * 128 + 128)
        rows = jnp.concatenate([source[:, cut], coef[:, cut].astype(F32)], axis=0)
        fine_payload[t] = rows.astype(BF16)
        target_out[t] = target[:, cut]
    for copy in copies[2:]:
        copy.wait()
    source, target = features(coarse_pts[...])
    for t in range(CT):
        halves = []
        for q in (2 * t, 2 * t + 1):
            mats = transfer[:, q * 128 : q * 128 + 128]
            left = jnp.dot(
                coef[:, q * 128 : q * 128 + 64], mats, preferred_element_type=F32
            )
            right = jnp.dot(
                coef[:, q * 128 + 64 : q * 128 + 128], mats, preferred_element_type=F32
            )
            halves.append(left[:, 0:64] + right[:, 64:128])
        cut = slice(t * 128, t * 128 + 128)
        rows = jnp.concatenate([source[:, cut], jnp.concatenate(halves, axis=1)], axis=0)
        coarse_payload[t] = rows.astype(BF16)
        target_out[FT + t] = target[:, cut]
    entries = [fine_list[...].astype(F32), coarse_list[...].astype(F32), jnp.zeros((8, 64), F32)]
    for n in range(2):
        part = entries[0] if n == 0 else jnp.concatenate(entries[1:], axis=0)
        coarse_payload[CT + n] = jnp.concatenate([part, jnp.zeros((16, 64), F32)], axis=1).astype(BF16)
    for slots, counts, at in ((fine_slots, fine_counts, 0), (coarse_slots, coarse_counts, FINE)):
        rows = slots.shape[0]
        wide = jnp.broadcast_to(counts[...].astype(F32), (128, rows)).T
        spot = lax.broadcasted_iota(jnp.int32, (rows, 128), 1)
        code = jnp.concatenate([slots[...], jnp.zeros((rows, 128 - PAIRS), jnp.int32)], axis=1)
        codes[at : at + rows] = jnp.where(spot.astype(F32) < wide, code, -1)


def prep(*arrays):
    vm = pl.BlockSpec(memory_space=pltpu.VMEM)
    kept = (0, 3)
    return pl.pallas_call(
        prep_kernel,
        out_shape=(
            jax.ShapeDtypeStruct((SIZES[0], 16, 128), BF16),
            jax.ShapeDtypeStruct((SIZES[1], 16, 128), BF16),
            jax.ShapeDtypeStruct((HALF, 40, 128), F32),
            jax.ShapeDtypeStruct((FINE + COARSE, 128), jnp.int32),
        )
        + tuple(jax.ShapeDtypeStruct(arrays[n].shape, arrays[n].dtype) for n in kept),
        in_specs=[pl.BlockSpec(memory_space=pltpu.HBM)] * len(arrays),
        out_specs=[vm] * 6,
        scratch_shapes=[
            pltpu.VMEM(array.shape, array.dtype)
            for n, array in enumerate(arrays)
            if n not in kept
        ]
        + [pltpu.SemaphoreType.DMA((len(arrays),))],
        compiler_params=pltpu.CompilerParams(vmem_limit_bytes=8 * 1024 * 1024),
        name="prep",
    )(*arrays)


def take(row, index):
    return jnp.take_along_axis(jnp.broadcast_to(row, index.shape), index, axis=1)


def slot_rows(lists, code, clusters, capacity, level, owner_slot):
    live = code >= 0
    v = jnp.maximum(code, 0)
    remote = jnp.maximum(v - clusters, 0)
    owner = remote // capacity
    entry = remote - owner * capacity
    found = jnp.zeros(code.shape, jnp.int32)
    for i in range(capacity):
        found = jnp.where(entry == i, take(lists[i : i + 1], owner), found)
    is_own = v < clusters
    cluster = jnp.where(is_own, v, found)
    base = jnp.where(is_own, owner_slot, (owner % 2) * CHIPS + owner // 2) * SIZES[level]
    row = jnp.where(live, base + cluster // 2, ENDS[level])
    spot = lax.broadcasted_iota(jnp.int32, code.shape, 1)
    turn = ((cluster + spot) % 2) * 64
    return row, turn


def list_part(tiles, n, leaf):
    lane = lax.broadcasted_iota(jnp.int32, (16, 128), 1)
    part = jnp.zeros((16, 128), F32)
    for e in range(2 * CHIPS):
        base = ((e % 2) * CHIPS + e // 2) * SIZES[0] + CT
        got = pltpu.roll(tiles[base + n].astype(F32), lax.rem(e - leaf + 128, 128), 1)
        part = jnp.where(lane == e, got, part)
    return part.astype(jnp.int32)


def gather_pair(tiles, picks, count, s, p, into):
    m = 2 * p
    lane = lax.broadcasted_iota(jnp.int32, (16, 128), 1)
    first = pltpu.roll(tiles[picks[s, m]], picks[count + s, m], 1)
    second = pltpu.roll(tiles[picks[s, m + 1]], picks[count + s, m + 1], 1)
    into[p] = jnp.where(lane < 64, first, second)


def gather_all(tiles, picks, count, s, into):
    for p in range(PAIRS // 2):
        gather_pair(tiles, picks, count, s, p, into)


def feats_of(target_feats, t):
    block = target_feats[t].T
    feats, bias = block[:, 0:32].astype(BF16), block[:, 32:33]
    return [(feats[cut], bias[cut]) for cut in (slice(0, 64), slice(64, 128))]


def run_targets(tiles, picks, count, order, targets, stage):
    totals = [None for _ in targets]
    waiting = []

    def flush():
        r, both, weights = waiting.pop(0)
        part = lax.dot_general(both, weights, NT, preferred_element_type=F32)
        totals[r] = part[8:16] if totals[r] is None else totals[r] + part[8:16]

    for r, (feats, bias) in enumerate(targets):
        source = stage[r % 2]
        for group in range(PAIRS // 4):
            p = group * 2
            both = jnp.concatenate([source[p], source[p + 1]], axis=1)
            exponent = lax.dot_general(
                feats,
                jnp.concatenate([both, both], axis=0),
                (((1,), (0,)), ((), ())),
                preferred_element_type=F32,
            )
            waiting.append((r, both, jnp.exp2(exponent + bias).astype(BF16)))
            if len(waiting) > LAG:
                flush()
            for n in range(2):
                gather_pair(tiles, picks, count, order[r + 1], p + n, stage[(r + 1) % 2])
    while waiting:
        flush()
    return totals


FLOWS = (
    (True, 1, 0, 4),
    (True, -1, 4, 8),
    (False, 1, 8, 13),
    (False, -1, 13, 18),
    (True, 1, 0, 7),
    (True, -1, 7, 13),
    (False, 1, 13, 23),
    (False, -1, 23, 32),
)


def spread_kernel(
    coarse_payload,
    fine_payload,
    coef,
    target_feats,
    codes,
    fine_table,
    probes,
    staged,
    coarse_out,
    coarse_table,
    coarse_staged,
    zeros,
    stage0,
    stage1,
    picks,
    link_recv,
    link_send,
    chip_recv,
    chip_send,
    z_recv,
    z_send,
    own_sem,
):
    leaf = lax.axis_index("leaf")
    z = lax.axis_index("probe")
    core = lax.rem(leaf, 2)
    chip = leaf // 2
    x = lax.rem(chip, NX)
    y = chip // NX

    def chip_at(xs, ys):
        return lax.rem(y + ys + NY, NY) * NX + lax.rem(x + xs + NX, NX)

    def leaf_at(xs, ys):
        return chip_at(xs, ys) * 2 + core

    twin = chip * 2 + (1 - core)
    barrier = pltpu.get_barrier_semaphore()
    peers = [leaf_at(1, 0), leaf_at(-1, 0), leaf_at(0, 1), leaf_at(0, -1), twin]
    for peer in peers:
        pl.semaphore_signal(barrier, 1, device_id={"leaf": peer}, device_id_type=MESH)
    for s in range(1, NZ):
        pl.semaphore_signal(
            barrier, 1, device_id={"probe": lax.rem(z + s, NZ)}, device_id_type=MESH
        )
    pl.semaphore_wait(barrier, len(peers) + NZ - 1)

    payloads, tables = (coarse_payload, fine_payload), (coarse_table, fine_table)

    def rows_of(level, which_chip, low, high):
        first = (core * CHIPS + which_chip) * SIZES[level] + low
        return tables[level].at[pl.ds(first, high - low)]

    zeros[...] = jnp.zeros_like(zeros)
    local = []
    for level in range(2):
        end = ENDS[level]
        local.append((payloads[level], rows_of(level, chip, 0, SIZES[level])))
        local.append((zeros, tables[level].at[end : end + PAD]))
    local = [pltpu.make_async_copy(a, b, own_sem.at[n]) for n, (a, b) in enumerate(local)]
    for copy in local:
        copy.start()
    own_coef = pltpu.make_async_copy(coef, probes.at[z], own_sem.at[4])
    own_coef.start()

    def share_bytes(sem, which_core, level):
        count = CHIPS * SIZES[level]
        block = tables[level].at[pl.ds(which_core * count, count)]
        pltpu.make_async_copy(block, block, sem).wait()

    def piece(f, i, j):
        _, sign, low, high = FLOWS[f]
        return rows_of(f // 4, chip_at(-sign * i, -sign * j), low, high)

    def source(f, i, j):
        _, _, low, high = FLOWS[f]
        own_piece = isinstance(j, int) and i == 0 and j == 0
        return payloads[f // 4].at[low:high] if own_piece else piece(f, i, j)

    def push(f, i, j, along_x):
        _, sign, _, _ = FLOWS[f]
        peer = leaf_at(sign, 0) if along_x else leaf_at(0, sign)
        slot = (i + 1, j) if along_x else (i, j + 1)
        pltpu.make_async_remote_copy(
            source(f, i, j),
            piece(f, i, j),
            link_send.at[f // 4],
            link_recv.at[f, slot[0], slot[1]],
            device_id={"leaf": peer},
            device_id_type=MESH,
        ).start()

    def share(f, i, j):
        pltpu.make_async_remote_copy(
            source(f, i, j),
            piece(f, i, j),
            chip_send.at[f // 4],
            chip_recv.at[f // 4],
            device_id={"leaf": twin},
            device_id_type=MESH,
        ).start()

    def visit(f, i, j, arrived):
        if arrived:
            part = piece(f, i, j)
            pltpu.make_async_copy(part, part, link_recv.at[f, i, j]).wait()
        more_y = NY - 1 > j
        if FLOWS[f][0]:
            if i < NX - 1:
                pl.when(j == 0)(lambda: push(f, i, j, True))
            pl.when(more_y)(lambda: push(f, i, j, False))
        else:
            if i == 0:
                pl.when(more_y)(lambda: push(f, i, j, False))
            if i < NX - 1:
                push(f, i, j, True)
        share(f, i, j)

    def wave(flows, t):
        for i in range(NX):
            j = t - i
            if isinstance(t, int):
                if 0 <= j < NY:
                    for f in flows:
                        visit(f, i, j, t > 0)
            else:

                @pl.when(jnp.logical_and(j >= 0, j < NY))
                def _():
                    for f in flows:
                        visit(f, i, j, True)

    early, late = range(4), range(4, 8)
    wave(early, 0)
    wave(late, 0)
    for s in range(1, NZ):
        pltpu.make_async_remote_copy(
            coef,
            probes.at[z],
            z_send,
            z_recv,
            device_id={"probe": lax.rem(z + s, NZ)},
            device_id_type=MESH,
        ).start()
    for t in range(1, NX + NY - 1):
        wave(early, t)
        if t >= NX + NY - 1 - LEAD:
            wave(late, t - (NX + NY - 2 - LEAD))
    for copy in local:
        copy.wait()
    share_bytes(chip_recv.at[0], 1 - core, 0)

    owner_slot = core * CHIPS + chip
    lists = [list_part(coarse_table, n, leaf) for n in range(2)]
    row, turn = slot_rows(lists[1], codes[FINE:], COARSE, 8, 0, owner_slot)
    coarse_staged[0:COARSE] = row
    coarse_staged[COARSE:] = turn
    move = pltpu.make_async_copy(coarse_staged, picks, own_sem.at[5])
    move.start()
    row, turn = slot_rows(lists[0], codes[0:FINE], FINE, 16, 1, owner_slot)
    staged[0:FINE] = row
    staged[FINE:] = turn
    move.wait()
    stage = (stage0, stage1)
    gather_all(coarse_table, picks, COARSE, 0, stage0)
    steps = NX + NY - 2 - LEAD
    each = COARSE // steps

    def body(n, carry):
        wave(late, n + LEAD + 1)
        order = [n * each + u for u in range(each)]
        order.append(jnp.minimum((n + 1) * each, COARSE - 1))
        targets = []
        for u in range(each // 2):
            targets += feats_of(target_feats, FT + n * (each // 2) + u)
        outs = run_targets(coarse_table, picks, COARSE, order, targets, stage)
        for u in range(each):
            coarse_out[n * each + u] = jnp.concatenate(
                [outs[u], jnp.zeros((8, RANK), F32)], axis=1
            )
        return carry

    lax.fori_loop(0, steps, body, 0)

    own_coef.wait()
    share_bytes(chip_recv.at[1], 1 - core, 1)
    for level in range(2):
        share_bytes(chip_send.at[level], core, level)
        sent = tables[level].at[0 : (CHIPS - 1) * SIZES[level]]
        pltpu.make_async_copy(sent, sent, link_send.at[level]).wait()
    others = probes.at[0 : NZ - 1]
    pltpu.make_async_copy(others, others, z_recv).wait()
    pltpu.make_async_copy(others, others, z_send).wait()


def spread(coarse_payload, fine_payload, coef, feats, codes):
    dma = pltpu.SemaphoreType.DMA
    vm = pl.BlockSpec(memory_space=pltpu.VMEM)
    return pl.pallas_call(
        spread_kernel,
        out_shape=(
            jax.ShapeDtypeStruct((ENDS[1] + PAD, 16, 128), BF16),
            jax.ShapeDtypeStruct((NZ,) + coef.shape, BF16),
            jax.ShapeDtypeStruct((2 * FINE, 128), jnp.int32),
            jax.ShapeDtypeStruct((COARSE, 8, 128), F32),
        ),
        in_specs=[vm] * 5,
        out_specs=[vm] * 4,
        scratch_shapes=[
            pltpu.VMEM((ENDS[0] + PAD, 16, 128), BF16),
            pltpu.VMEM((2 * COARSE, 128), jnp.int32),
            pltpu.VMEM((PAD, 16, 128), BF16),
            pltpu.VMEM((PAIRS // 2, 16, 128), BF16),
            pltpu.VMEM((PAIRS // 2, 16, 128), BF16),
            pltpu.SMEM((2 * COARSE, 128), jnp.int32),
            dma((8, NX, NY)),
            dma((2,)),
            dma((2,)),
            dma((2,)),
            dma(()),
            dma(()),
            dma((6,)),
        ],
        compiler_params=pltpu.CompilerParams(
            collective_id=0, has_side_effects=True, vmem_limit_bytes=SPREAD_LIMIT
        ),
        name="spread",
    )(coarse_payload, fine_payload, coef, feats, codes)


def sweep_kernel(
    staged, tiles, target_feats, probes, transfer, coarse, far, partial, stage0, stage1, picks, sem
):
    z = lax.axis_index("probe")
    move = pltpu.make_async_copy(staged, picks, sem)
    move.start()
    move.wait()
    stage = (stage0, stage1)
    gather_all(tiles, picks, FINE, 0, stage0)

    def step(n, carry):
        order = [n * EACH + u for u in range(EACH)]
        order.append(jnp.minimum((n + 1) * EACH, FINE - 1))
        targets = []
        for u in range(EACH // 2):
            targets += feats_of(target_feats, n * (EACH // 2) + u)
        outs = run_targets(tiles, picks, FINE, order, targets, stage)
        for u in range(EACH // 2):
            q = n * (EACH // 2) + u
            cut = pl.ds(pl.multiple_of(q * 128, 128), 128)
            mats = transfer[:, cut]
            up = coarse[q]
            spread_up = jnp.concatenate([up, pltpu.roll(up, RANK, 1)], axis=0).astype(BF16)
            down = lax.dot_general(spread_up, mats, NT, preferred_element_type=F32)
            low, high = outs[2 * u : 2 * u + 2]
            far[:, cut] = jnp.concatenate([low + down[0:8], high + down[8:16]], axis=1)
        return carry

    lax.fori_loop(0, FINE // EACH, step, 0)

    whole = far[...]
    first = whole.astype(BF16)
    rest = whole - first.astype(F32)
    second = rest.astype(BF16)
    third = (rest - second.astype(F32)).astype(BF16)
    coefs = probes[...].reshape(NZ * 8, FINE * RANK)
    gram = (
        lax.dot_general(coefs, first, NT, preferred_element_type=F32)
        + lax.dot_general(coefs, second, NT, preferred_element_type=F32)
        + lax.dot_general(coefs, third, NT, preferred_element_type=F32)
    )
    wide = jnp.concatenate([gram, jnp.zeros((NZ * 8, 120), F32)], axis=1)
    partial[...] = pltpu.roll(wide, z * 8, 1)


def sweep(staged, table, feats, probes, transfer, coarse):
    vm = pl.BlockSpec(memory_space=pltpu.VMEM)
    return pl.pallas_call(
        sweep_kernel,
        out_shape=(
            jax.ShapeDtypeStruct((8, FINE * RANK), F32),
            jax.ShapeDtypeStruct((NZ * 8, 128), F32),
        ),
        in_specs=[vm] * 6,
        out_specs=[vm, vm],
        scratch_shapes=[
            pltpu.VMEM((PAIRS // 2, 16, 128), BF16),
            pltpu.VMEM((PAIRS // 2, 16, 128), BF16),
            pltpu.SMEM((2 * FINE, 128), jnp.int32),
            pltpu.SemaphoreType.DMA(()),
        ],
        compiler_params=pltpu.CompilerParams(vmem_limit_bytes=SWEEP_LIMIT),
        name="sweep",
    )(staged, table, feats, probes, transfer, coarse)


def reduce_kernel(gram_scale, partial, out, at_z, at_x, at_y, work, recv, send):
    leaf = lax.axis_index("leaf")
    z = lax.axis_index("probe")
    inner = lax.rem(leaf, 2 * NX)
    y = leaf // (2 * NX)

    def z_peer(s):
        return {"probe": lax.rem(z + s, NZ)}

    def x_peer(s):
        return {"leaf": y * (2 * NX) + lax.rem(inner + s, 2 * NX)}

    def y_peer(s):
        return {"leaf": lax.rem(y + s, NY) * (2 * NX) + inner}

    barrier = pltpu.get_barrier_semaphore()
    for peer in (z_peer, x_peer, y_peer):
        for s in range(1, 8):
            pl.semaphore_signal(barrier, 1, device_id=peer(s), device_id_type=MESH)
    pl.semaphore_wait(barrier, 21)

    def exchange(stage, peer, me, source, buffer):
        for s in range(1, 8):
            pltpu.make_async_remote_copy(
                source(s),
                buffer.at[me],
                send.at[stage],
                recv.at[stage],
                device_id=peer(s),
                device_id_type=MESH,
            ).start()
        buffer[me] = source(0)[...]
        got = buffer.at[0:7]
        pltpu.make_async_copy(got, got, recv.at[stage]).wait()
        total = buffer[0]
        for n in range(1, 8):
            total = total + buffer[n]
        pltpu.make_async_copy(got, got, send.at[stage]).wait()
        return total

    work[0] = exchange(0, z_peer, z, lambda s: partial.at[lax.rem(z + s, NZ)], at_z)
    work[1] = exchange(1, x_peer, inner, lambda s: work.at[0], at_x)
    out[...] = exchange(2, y_peer, y, lambda s: work.at[1], at_y) * gram_scale


def reduce_gram(partial, gram_scale):
    vm = pl.BlockSpec(memory_space=pltpu.VMEM)
    return pl.pallas_call(
        functools.partial(reduce_kernel, gram_scale),
        out_shape=jax.ShapeDtypeStruct((8, 128), F32),
        in_specs=[vm],
        out_specs=vm,
        scratch_shapes=[
            pltpu.VMEM((8, 8, 128), F32),
            pltpu.VMEM((8, 8, 128), F32),
            pltpu.VMEM((8, 8, 128), F32),
            pltpu.VMEM((2, 8, 128), F32),
            pltpu.SemaphoreType.DMA((3,)),
            pltpu.SemaphoreType.DMA((3,)),
        ],
        compiler_params=pltpu.CompilerParams(
            collective_id=1, has_side_effects=True, vmem_limit_bytes=1024 * 1024
        ),
        name="reduce_gram",
    )(partial)


def shards(
    coef_fine,
    points_fine,
    points_coarse,
    transfer,
    send_fine,
    slots_fine,
    counts_fine,
    send_coarse,
    slots_coarse,
    counts_coarse,
):
    arrays = (
        coef_fine,
        points_fine,
        points_coarse,
        transfer,
        send_fine[0].T,
        send_coarse[0].T,
        slots_fine,
        slots_coarse,
        counts_fine.reshape(1, FINE),
        counts_coarse.reshape(1, COARSE),
    )
    coarse_payload, fine_payload, feats, codes, coef, mats = prep(
        *[pltpu.with_memory_space_constraint(array, pltpu.HBM) for array in arrays]
    )
    table, probes, staged, coarse = spread(coarse_payload, fine_payload, coef, feats, codes)
    far, partial = sweep(staged, table, feats, probes, mats, coarse)
    gram_scale = 1.0 / math.sqrt(2 * CHIPS * FINE * RANK)
    gram = reduce_gram(partial.reshape(NZ, 8, 128), gram_scale)
    return (far, gram[:, 0 : NZ * 8])


def solution(mesh):
    return jax.shard_map(
        shards,
        mesh=mesh,
        in_specs=(
            P("probe", "leaf"),
            P(None, "leaf"),
            P(None, "leaf"),
            P(None, "leaf"),
            P("leaf", None, None),
            P("leaf", None),
            P("leaf"),
            P("leaf", None, None),
            P("leaf", None),
            P("leaf"),
        ),
        out_specs=(P("probe", "leaf"), P("probe", None)),
        check_vma=False,
    )
```

time: 124 us -> 124 us (level)
  Pallas kernels: 111 us -> 122 us
  local copies, waits for them, and re-layouts: 11.4 us -> 0.6 us
    pallas_call x2, Pallas kernels: 60.8 us -> 84.6 us  [the longest x1 82.8 us: spread(): pl.pallas_call(spread_kernel, out_shape=(jax.ShapeDtypeStruct((ENDS[1] +...]
    pallas_call x1, Pallas kernels: 32.8 us -> 20.9 us  [sweep(): pl.pallas_call(sweep_kernel, out_shape=(jax.ShapeDtypeStruct((8, FINE * R...]
    unnamed x27 -> x1, local copies, waits for them, and re-layouts: 11.4 us -> 0.6 us
where the time goes in v3:
time: 124 us
  Pallas kernels  122 us (98%)
    pallas_call x1, Pallas kernels, spread(): pl.pallas_call(spread_kernel, out_shape=(jax.ShapeDtypeStruct((ENDS[1] +...  82.8 us
    pallas_call x1, Pallas kernels, sweep(): pl.pallas_call(sweep_kernel, out_shape=(jax.ShapeDtypeStruct((8, FINE * R...  20.9 us
    pallas_call x1, Pallas kernels, reduce_gram(): pl.pallas_call(functools.partial(reduce_kernel, gram_scale), out_shape=ja...  16.8 us

profile of v3, /device:TPU:1, one launch (start us, length us, event | category | flops | bytes accessed | tf_op | source)
XLA Modules:
  0.0 123.6 jit_solution(8096710834830023977)
XLA Ops:
  0.6 1.8 %prep.1 = (bf16[18,16,128]{2,1,0:T(8,128)(2,1)S(1)}, bf16[32,16,128]{2,1,0:T(8,128)(2,1)S(1)}, f32[48,40,128]{2,1,0:T(8,128)S(1)}, s32[96,128]{1,0:T(8,128)S(1)}...) custom-call(bf16[8,4096]{1,0:T(8,128)(2,1)} %coef_in.1, f32[3,4096]{1,0:T(4,128)} %fine_pts_in.1, ...), custom_call_target="tpu_custom_call" | custom-call | tf_op jit(solution)/shard_map/prep/pallas_call | solution.py:147
  2.5 82.8 %spread.1 = (bf16[2056,16,128]{2,1,0:T(8,128)(2,1)S(1)}, bf16[8,8,4096]{2,1,0:T(8,128)(2,1)S(1)}, s32[128,128]{1,0:T(8,128)S(1)}, f32[32,8,128]{2,1,0:T(8,128)S(1)}) custom-call(bf16[18,16,128]{2,1,0:T(8,128)(2,1)S(1)} %get-tuple-element.14.coarse_payload, bf16[32,16,128]{2,1,0:T(8,128)(2,1)S(1)} %get-tuple-element.15.fine_payload, ...), custom_call_target="tpu_custom_call" | custom-call | tf_op jit(solution)/shard_map/spread/pallas_call | solution.py:461
  85.3 20.9 %sweep.1 = (f32[8,4096]{1,0:T(8,128)}, f32[64,128]{1,0:T(8,128)S(1)}) custom-call(s32[128,128]{1,0:T(8,128)S(1)} %get-tuple-element.19.staged, bf16[2056,16,128]{2,1,0:T(8,128)(2,1)S(1)} %get-tuple-element.20.tiles, f32[48,40,128]{2,1,0:T(8,128)S(1)} %get-tuple-element.17.target_feats, bf16[8,8,4096]{2,1,0:T(8,128)(2,1)S(1)} %get-tuple-element.21.probes, ...), custom_call_target="tpu_custom_call" | custom-call | tf_op jit(solution)/shard_map/sweep/pallas_call | solution.py:540
  106.2 16.8 %reduce_gram.1 = f32[8,128]{1,0:T(8,128)S(1)} custom-call(f32[8,8,128]{2,1,0:T(8,128)S(1)} %bitcast.10), custom_call_target="tpu_custom_call" | custom-call | tf_op jit(solution)/shard_map/reduce_gram/pallas_call | solution.py:606
  123.0 0.6 copy.13

commit v4 on v3

--- a/solution.py
+++ b/solution.py
@@ -22,8 +22,30 @@
 MESH = pl.DeviceIdType.MESH
 F32, BF16 = jnp.float32, jnp.bfloat16
 LAG = 12
-LEAD = 2
 EACH = 16
+X_TREE = {1: 0, 2: 1, -1: 0}
+Y_TREE = {1: 0, 2: 1, 3: 2, 4: 3, -1: 0, -2: -1, -3: -2}
+COARSE_WAVE, FINE_WAVE, COMPUTE = 0, 1, 2
+SCHEDULE = (
+    (COARSE_WAVE, 0),
+    (FINE_WAVE, 0),
+    (COARSE_WAVE, 1),
+    (COARSE_WAVE, 2),
+    (FINE_WAVE, 1),
+    (COARSE_WAVE, 3),
+    (COARSE_WAVE, 4),
+    (FINE_WAVE, 2),
+    (COARSE_WAVE, 5),
+    (COARSE_WAVE, 6),
+    (FINE_WAVE, 3),
+    (COMPUTE, 3),
+    (FINE_WAVE, 4),
+    (COMPUTE, 3),
+    (FINE_WAVE, 5),
+    (COMPUTE, 2),
+    (FINE_WAVE, 6),
+)
+CHUNK = 4
 NT = (((1,), (1,)), ((), ()))
 TABLE_SPACE = pltpu.VMEM
 SPREAD_LIMIT = 20 * 1024 * 1024
@@ -259,6 +281,10 @@
 )
 
 
+def children(tree, offset):
+    return [child - offset for child, parent in tree.items() if parent == offset]
+
+
 def spread_kernel(
     coarse_payload,
     fine_payload,
@@ -336,18 +362,17 @@
 
     def source(f, i, j):
         _, _, low, high = FLOWS[f]
-        own_piece = isinstance(j, int) and i == 0 and j == 0
-        return payloads[f // 4].at[low:high] if own_piece else piece(f, i, j)
-
-    def push(f, i, j, along_x):
-        _, sign, _, _ = FLOWS[f]
-        peer = leaf_at(sign, 0) if along_x else leaf_at(0, sign)
-        slot = (i + 1, j) if along_x else (i, j + 1)
+        return payloads[f // 4].at[low:high] if i == 0 and j == 0 else piece(f, i, j)
+
+    def push(f, i, j, along_x, hop):
+        step = FLOWS[f][1] * hop
+        peer = leaf_at(step, 0) if along_x else leaf_at(0, step)
+        slot = (i + hop, j) if along_x else (i, j + hop)
         pltpu.make_async_remote_copy(
             source(f, i, j),
             piece(f, i, j),
             link_send.at[f // 4],
-            link_recv.at[f, slot[0], slot[1]],
+            link_recv.at[f, slot[0] + 1, slot[1] + 3],
             device_id={"leaf": peer},
             device_id_type=MESH,
         ).start()
@@ -362,39 +387,26 @@
             device_id_type=MESH,
         ).start()
 
-    def visit(f, i, j, arrived):
-        if arrived:
+    def visit(f, i, j):
+        if i != 0 or j != 0:
             part = piece(f, i, j)
-            pltpu.make_async_copy(part, part, link_recv.at[f, i, j]).wait()
-        more_y = NY - 1 > j
-        if FLOWS[f][0]:
-            if i < NX - 1:
-                pl.when(j == 0)(lambda: push(f, i, j, True))
-            pl.when(more_y)(lambda: push(f, i, j, False))
-        else:
-            if i == 0:
-                pl.when(more_y)(lambda: push(f, i, j, False))
-            if i < NX - 1:
-                push(f, i, j, True)
+            pltpu.make_async_copy(part, part, link_recv.at[f, i + 1, j + 3]).wait()
+        x_first = FLOWS[f][0]
+        if x_first or i == 0:
+            for hop in children(Y_TREE, j):
+                push(f, i, j, False, hop)
+        if not x_first or j == 0:
+            for hop in children(X_TREE, i):
+                push(f, i, j, True, hop)
         share(f, i, j)
 
-    def wave(flows, t):
-        for i in range(NX):
-            j = t - i
-            if isinstance(t, int):
-                if 0 <= j < NY:
-                    for f in flows:
-                        visit(f, i, j, t > 0)
-            else:
-
-                @pl.when(jnp.logical_and(j >= 0, j < NY))
-                def _():
-                    for f in flows:
-                        visit(f, i, j, True)
-
-    early, late = range(4), range(4, 8)
-    wave(early, 0)
-    wave(late, 0)
+    def wave(level, t):
+        for i in range(-1, NX - 1):
+            for j in range(-3, NY - 3):
+                if abs(i) + abs(j) == t:
+                    for f in range(4 * level, 4 * level + 4):
+                        visit(f, i, j)
+
     for s in range(1, NZ):
         pltpu.make_async_remote_copy(
             coef,
@@ -404,45 +416,47 @@
             device_id={"probe": lax.rem(z + s, NZ)},
             device_id_type=MESH,
         ).start()
-    for t in range(1, NX + NY - 1):
-        wave(early, t)
-        if t >= NX + NY - 1 - LEAD:
-            wave(late, t - (NX + NY - 2 - LEAD))
-    for copy in local:
-        copy.wait()
-    share_bytes(chip_recv.at[0], 1 - core, 0)
-
-    owner_slot = core * CHIPS + chip
-    lists = [list_part(coarse_table, n, leaf) for n in range(2)]
-    row, turn = slot_rows(lists[1], codes[FINE:], COARSE, 8, 0, owner_slot)
-    coarse_staged[0:COARSE] = row
-    coarse_staged[COARSE:] = turn
-    move = pltpu.make_async_copy(coarse_staged, picks, own_sem.at[5])
-    move.start()
-    row, turn = slot_rows(lists[0], codes[0:FINE], FINE, 16, 1, owner_slot)
-    staged[0:FINE] = row
-    staged[FINE:] = turn
-    move.wait()
     stage = (stage0, stage1)
-    gather_all(coarse_table, picks, COARSE, 0, stage0)
-    steps = NX + NY - 2 - LEAD
-    each = COARSE // steps
+    begun = 0
+
+    def start_compute():
+        for copy in local:
+            copy.wait()
+        share_bytes(chip_recv.at[0], 1 - core, 0)
+        owner_slot = core * CHIPS + chip
+        lists = [list_part(coarse_table, n, leaf) for n in range(2)]
+        row, turn = slot_rows(lists[1], codes[FINE:], COARSE, 8, 0, owner_slot)
+        coarse_staged[0:COARSE] = row
+        coarse_staged[COARSE:] = turn
+        move = pltpu.make_async_copy(coarse_staged, picks, own_sem.at[5])
+        move.start()
+        row, turn = slot_rows(lists[0], codes[0:FINE], FINE, 16, 1, owner_slot)
+        staged[0:FINE] = row
+        staged[FINE:] = turn
+        move.wait()
+        gather_all(coarse_table, picks, COARSE, 0, stage0)
 
     def body(n, carry):
-        wave(late, n + LEAD + 1)
-        order = [n * each + u for u in range(each)]
-        order.append(jnp.minimum((n + 1) * each, COARSE - 1))
+        order = [n * CHUNK + u for u in range(CHUNK)]
+        order.append(jnp.minimum((n + 1) * CHUNK, COARSE - 1))
         targets = []
-        for u in range(each // 2):
-            targets += feats_of(target_feats, FT + n * (each // 2) + u)
+        for u in range(CHUNK // 2):
+            targets += feats_of(target_feats, FT + n * (CHUNK // 2) + u)
         outs = run_targets(coarse_table, picks, COARSE, order, targets, stage)
-        for u in range(each):
-            coarse_out[n * each + u] = jnp.concatenate(
+        for u in range(CHUNK):
+            coarse_out[n * CHUNK + u] = jnp.concatenate(
                 [outs[u], jnp.zeros((8, RANK), F32)], axis=1
             )
         return carry
 
-    lax.fori_loop(0, steps, body, 0)
+    for kind, count in SCHEDULE:
+        if kind != COMPUTE:
+            wave(kind, count)
+            continue
+        if begun == 0:
+            start_compute()
+        lax.fori_loop(begun, begun + count, body, 0)
+        begun += count
 
     own_coef.wait()
     share_bytes(chip_recv.at[1], 1 - core, 1)

time: 124 us -> 104 us (0.84)
  Pallas kernels: 122 us -> 103 us
    pallas_call x1, Pallas kernels: 82.8 us -> 63 us  [spread(): pl.pallas_call(spread_kernel, out_shape=(jax.ShapeDtypeStruct((ENDS[1] +...]
where the time goes in v4:
time: 104 us
  Pallas kernels  103 us (99%)
    pallas_call x1, Pallas kernels, spread(): pl.pallas_call(spread_kernel, out_shape=(jax.ShapeDtypeStruct((ENDS[1] +...  63 us
    pallas_call x1, Pallas kernels, sweep(): pl.pallas_call(sweep_kernel, out_shape=(jax.ShapeDtypeStruct((8, FINE * R...  21.1 us
    pallas_call x1, Pallas kernels, reduce_gram(): pl.pallas_call(functools.partial(reduce_kernel, gram_scale), out_shape=ja...  16.7 us

profile of v4, /device:TPU:1, one launch (start us, length us, event | category | flops | bytes accessed | tf_op | source)
XLA Modules:
  0.0 104.0 jit_solution(4131700011851138631)
XLA Ops:
  0.6 1.8 %prep.1 = (bf16[18,16,128]{2,1,0:T(8,128)(2,1)S(1)}, bf16[32,16,128]{2,1,0:T(8,128)(2,1)S(1)}, f32[48,40,128]{2,1,0:T(8,128)S(1)}, s32[96,128]{1,0:T(8,128)S(1)}...) custom-call(bf16[8,4096]{1,0:T(8,128)(2,1)} %coef_in.1, f32[3,4096]{1,0:T(4,128)} %fine_pts_in.1, ...), custom_call_target="tpu_custom_call" | custom-call | tf_op jit(solution)/shard_map/prep/pallas_call | solution.py:169
  2.5 63.0 %spread.1 = (bf16[2056,16,128]{2,1,0:T(8,128)(2,1)S(1)}, bf16[8,8,4096]{2,1,0:T(8,128)(2,1)S(1)}, s32[128,128]{1,0:T(8,128)S(1)}, f32[32,8,128]{2,1,0:T(8,128)S(1)}) custom-call(bf16[18,16,128]{2,1,0:T(8,128)(2,1)S(1)} %get-tuple-element.14.coarse_payload, bf16[32,16,128]{2,1,0:T(8,128)(2,1)S(1)} %get-tuple-element.15.fine_payload, ...), custom_call_target="tpu_custom_call" | custom-call | tf_op jit(solution)/shard_map/spread/pallas_call | solution.py:475
  65.5 21.1 %sweep.1 = (f32[8,4096]{1,0:T(8,128)}, f32[64,128]{1,0:T(8,128)S(1)}) custom-call(s32[128,128]{1,0:T(8,128)S(1)} %get-tuple-element.19.staged, bf16[2056,16,128]{2,1,0:T(8,128)(2,1)S(1)} %get-tuple-element.20.tiles, f32[48,40,128]{2,1,0:T(8,128)S(1)} %get-tuple-element.17.target_feats, bf16[8,8,4096]{2,1,0:T(8,128)(2,1)S(1)} %get-tuple-element.21.probes, ...), custom_call_target="tpu_custom_call" | custom-call | tf_op jit(solution)/shard_map/sweep/pallas_call | solution.py:554
  86.7 16.7 %reduce_gram.1 = f32[8,128]{1,0:T(8,128)S(1)} custom-call(f32[8,8,128]{2,1,0:T(8,128)S(1)} %bitcast.10), custom_call_target="tpu_custom_call" | custom-call | tf_op jit(solution)/shard_map/reduce_gram/pallas_call | solution.py:620
  103.4 0.6 copy.13
